TPU v7x, 128 devices: a whole 4x4x4 slice. The times are simulated.
128 devices in a mesh: req: 32 (over x, y, z_hi), rep: 4 (over z_lo, core).
Axes of the slice: x: 4, y: 4, z: 4 (z_hi: 2, z_lo: 2; z = z_hi * 2 + z_lo), core: 2. Of those that a mesh axis runs over, the one named last changes fastest.
Arguments:
- tokens: bfloat16 [128, 2, 2048], P('req'), may hold values from -6 to 6
- norm_gains: float32 [2, 2048], replicated, may hold values from 0.1 to 1.9
- w_kv: bfloat16 [2048, 2, 2048], P(None, None, 'rep'), may hold values from -0.125 to 0.125
- w_query: bfloat16 [32, 2048, 512], P('req', None, 'rep'), may hold values from -0.125 to 0.125
- w_out: bfloat16 [32, 512, 2048], P('req', 'rep'), may hold values from -0.5 to 0.5
- w_gate: bfloat16 [32, 2048, 1408], P('req', None, 'rep'), may hold values from -0.125 to 0.125
- w_up: bfloat16 [32, 2048, 1408], P('req', None, 'rep'), may hold values from -0.125 to 0.125
- w_down: bfloat16 [32, 1408, 2048], P('req', 'rep'), may hold values from -0.078125 to 0.078125
- kv_pages: bfloat16 [8192, 16, 2, 2048], P('req', None, None, 'rep'), may hold values from -80 to 80
- page_table: int32 [128, 64], P('req'), may hold values from 0 to 255, as said below
- cache_len: int32 [128], P('req'), may hold values from 1 to 1024
- route_ids: int32 [128, 2, 2, 2], P('req'), may hold values from 0 to 7, all different within a row
- route_gates: bfloat16 [128, 2, 2, 2], P('req'), may hold values from 0.19921875 to 1
- new_slot: int32 [128], P('req'), may hold values from 0 to 127, each once
Outputs:
- layer_out: bfloat16 [128, 2, 2048], P('req')
Inputs may be any that keep to these rules, and one draw needn't show every extreme that they name: `page_table`: row i lists 64 distinct pages of the pool of the device that holds request i; two requests of one device share no page.
All inputs are finite; a program needn't handle non-finite values.
Results may differ from a plain program's by a relative error of at most 0.022.
Values may be sent and summed in bfloat16 or wider, within the bound.
No kernel may reach another device: no remote copies, remote signals or barrier semaphores. Data moves between devices by JAX's collectives and lax.ppermute only.
A program may use at most 128 MiB of HBM per device.

v0:
```python
import math

import jax
import jax.numpy as jnp
from jax import lax
from jax.sharding import PartitionSpec as P

HD = 128
EXPERTS = 8


EPSILON = 1e-06
MASKED = -1e30


def normalize(values, gain_row):
    scaling = lax.rsqrt(jnp.mean(values * values, axis=-1, keepdims=True) + EPSILON)
    return (values * scaling * gain_row).astype(jnp.bfloat16)


def expert_share(ids_block, gates_block, expert):
    return jnp.sum(jnp.where(ids_block == expert, gates_block.astype(jnp.float32), 0.0), axis=-1)


def attend(queries, cache_keys, cache_values, lengths, extra_keys, extra_values, extra_live):
    inv_scale = 1.0 / math.sqrt(queries.shape[-1])
    cache_scores = (
        jnp.einsum("jskhc,jlhc->jskhl", queries, cache_keys, preferred_element_type=jnp.float32)
        * inv_scale
    )
    alive_mask = jnp.arange(cache_keys.shape[1], dtype=jnp.int32)[None, :] < lengths[:, None]
    cache_scores = jnp.where(alive_mask[:, None, None, None, :], cache_scores, MASKED)
    extra_scores = (
        jnp.einsum("jskhc,jxhc->jskhx", queries, extra_keys, preferred_element_type=jnp.float32)
        * inv_scale
    )
    extra_scores = jnp.where(extra_live[None, :, None, None, :], extra_scores, MASKED)
    highest = jnp.maximum(jnp.max(cache_scores, axis=-1), jnp.max(extra_scores, axis=-1))[..., None]
    cache_exp = jnp.exp(cache_scores - highest)
    extra_exp = jnp.exp(extra_scores - highest)
    denominator = (jnp.sum(cache_exp, axis=-1) + jnp.sum(extra_exp, axis=-1))[..., None]
    cache_weight = (cache_exp / denominator).astype(jnp.bfloat16)
    extra_weight = (extra_exp / denominator).astype(jnp.bfloat16)
    mixture = jnp.einsum(
        "jskhl,jlhc->jskhc", cache_weight, cache_values, preferred_element_type=jnp.float32
    )
    mixture = mixture + jnp.einsum(
        "jskhx,jxhc->jskhc", extra_weight, extra_values, preferred_element_type=jnp.float32
    )
    return mixture.astype(jnp.bfloat16)


def combine(term_fn, all_rows):
    partial_value = lax.psum_scatter(
        term_fn(jnp.int32(0), all_rows // lax.axis_size("req") * lax.axis_size("req")).astype(
            jnp.bfloat16
        ),
        "req",
        scatter_dimension=0,
        tiled=True,
    )
    return lax.psum(partial_value, "rep").astype(jnp.float32)


def shards(
    tokens,
    norm_gains,
    w_kv,
    w_query,
    w_out,
    w_gate,
    w_up,
    w_down,
    kv_pages,
    page_table,
    cache_len,
    route_ids,
    route_gates,
    new_slot,
):
    rows_dev = tokens.shape[0]
    req_count = lax.axis_size("req")
    all_rows = rows_dev * req_count
    holders = req_count // EXPERTS
    expert = lax.axis_index("req") // holders
    head_dim = HD
    heads_rep = kv_pages.shape[-1] // head_dim
    heads_dev = w_query.shape[-1] // head_dim
    inputs = tokens.astype(jnp.float32)
    normed = normalize(inputs, norm_gains[0])
    cache_pages = kv_pages[page_table].reshape(rows_dev, -1, 2, heads_rep, head_dim)
    cache_keys = cache_pages[:, :, 0]
    cache_values = cache_pages[:, :, 1]
    experts_row = jnp.arange(EXPERTS, dtype=jnp.int32)

    def fresh_kv(normed_rows):
        return jnp.einsum(
            "jd,dtc->jtc", normed_rows, w_kv, preferred_element_type=jnp.float32
        ).astype(jnp.bfloat16)

    def pair_kv(first_kv, second_kv):
        return jnp.stack([first_kv, second_kv], axis=1).reshape(rows_dev, 2, 2, heads_rep, head_dim)

    first_fresh = fresh_kv(normed[:, 0])

    def section(step_list, gathered, slot_map, all_ids, all_gates, extra_kv):
        step_count = len(step_list)
        first_step = step_list[0]
        step_span = slice(first_step, first_step + step_count)
        inverse = (
            jnp.zeros((all_rows,), jnp.int32)
            .at[slot_map]
            .set(jnp.arange(all_rows, dtype=jnp.int32))
        )
        queries = jnp.einsum(
            "bsd,dc->bsc", gathered, w_query[0], preferred_element_type=jnp.float32
        ).astype(jnp.bfloat16)
        columns = []
        own_ids = []
        for position, current in enumerate(step_list):
            if current == 0:
                columns.append(queries[:, position])
                own_ids.append(route_ids[:, 0, 0])
            else:
                columns.append(jnp.take(queries[:, position], slot_map, axis=0))
                own_ids.append(jnp.take(all_ids[:, 0, 1], new_slot, axis=0))
        ordered = jnp.stack(columns, axis=1).reshape(
            req_count, rows_dev, step_count, heads_dev * head_dim
        )
        arrived = lax.all_to_all(ordered, "req", split_axis=0, concat_axis=0, tiled=True)
        arrived = arrived.reshape(EXPERTS, holders, rows_dev, step_count, heads_dev, head_dim)
        chosen = (jnp.stack(own_ids, axis=1)[..., None] == experts_row).astype(jnp.bfloat16)
        picked = jnp.einsum(
            "jske,egjshc->jskghc", chosen, arrived, preferred_element_type=jnp.float32
        ).astype(jnp.bfloat16)
        picked = picked.reshape(rows_dev, step_count, 2, heads_rep, head_dim)
        extra_live = jnp.array(
            [[extra_slot <= current for extra_slot in range(2)] for current in step_list]
        )
        result = attend(
            picked,
            cache_keys,
            cache_values,
            cache_len,
            extra_kv[:, :, 0],
            extra_kv[:, :, 1],
            extra_live,
        )
        result = result.reshape(rows_dev, step_count, 2, holders, heads_dev, head_dim)
        spread = jnp.einsum(
            "jske,jskghc->egjshc", chosen, result, preferred_element_type=jnp.float32
        ).astype(jnp.bfloat16)
        returned = lax.all_to_all(
            spread.reshape(req_count, rows_dev, step_count, heads_dev * head_dim),
            "req",
            split_axis=0,
            concat_axis=0,
            tiled=True,
        )
        returned = returned.reshape(all_rows, step_count, heads_dev * head_dim)
        answers = jnp.stack(
            [
                (
                    returned[:, position]
                    if current == 0
                    else jnp.take(returned[:, position], inverse, axis=0)
                )
                for position, current in enumerate(step_list)
            ],
            axis=1,
        )
        attn_share = expert_share(all_ids[:, 0, step_span], all_gates[:, 0, step_span], expert)
        ffn_share = expert_share(all_ids[:, 1, step_span], all_gates[:, 1, step_span], expert)

        def attn_term(first_row, row_count):
            return (
                jnp.einsum("bsc,cd->bsd", answers, w_out[0], preferred_element_type=jnp.float32)
                * attn_share[..., None]
            )

        hidden = inputs[:, step_span] + combine(attn_term, all_rows)
        hidden_normed = normalize(hidden, norm_gains[1])
        block_rows = lax.all_gather(hidden_normed, "req", axis=0, tiled=True)
        gate_part = jnp.einsum(
            "bsd,df->bsf", block_rows, w_gate[0], preferred_element_type=jnp.float32
        )
        up_part = jnp.einsum("bsd,df->bsf", block_rows, w_up[0], preferred_element_type=jnp.float32)
        hidden_units = (jax.nn.silu(gate_part) * up_part).astype(jnp.bfloat16)

        def ffn_term(first_row, row_count):
            return (
                jnp.einsum(
                    "bsf,fd->bsd", hidden_units, w_down[0], preferred_element_type=jnp.float32
                )
                * ffn_share[..., None]
            )

        return (hidden + combine(ffn_term, all_rows)).astype(jnp.bfloat16)

    first_rows, all_ids, all_gates, slot_map = (
        lax.all_gather(normed[:, 0:1], "req", axis=0, tiled=True),
        lax.all_gather(route_ids, "req", axis=0, tiled=True),
        lax.all_gather(route_gates, "req", axis=0, tiled=True),
        lax.all_gather(new_slot, "req", axis=0, tiled=True),
    )
    early = section(
        (0,), first_rows, slot_map, all_ids, all_gates, pair_kv(first_fresh, first_fresh)
    )
    second_rows = lax.all_gather(normed[:, 1:2], "req", axis=0, tiled=True)
    second_fresh = fresh_kv(jnp.take(second_rows[:, 0], new_slot, axis=0))
    later = section(
        (1,), second_rows, slot_map, all_ids, all_gates, pair_kv(first_fresh, second_fresh)
    )
    return jnp.concatenate([early, later], axis=1)


def solution(mesh):
    in_specs = (
        P("req", None, None),
        P(),
        P(None, None, "rep"),
        P("req", None, "rep"),
        P("req", "rep", None),
        P("req", None, "rep"),
        P("req", None, "rep"),
        P("req", "rep", None),
        P("req", None, None, "rep"),
        P("req", None),
        P("req"),
        P("req", None, None, None),
        P("req", None, None, None),
        P("req"),
    )
    out_specs = P("req", None, None)
    return jax.shard_map(shards, mesh=mesh, in_specs=in_specs, out_specs=out_specs, check_vma=False)
```

profile of v0, /device:TPU:1, one launch (start us, length us, event | category | flops | bytes accessed | tf_op | source)
XLA Modules:
  0.0 1477.4 jit_solution(3638717455090007884)
XLA Ops:
  6.5 1.0 multiply_reduce_fusion
  7.5 0.8 fusion.155
  8.3 0.8 multiply_convert_fusion
  9.2 88.1 %all_gather.21 = bf16[128,1,2048]{2,1,0:T(2,128)(2,1)S(1)} all-gather(bf16[4,1,2048]{2,1,0:T(2,128)(2,1)S(1)} %copy.217), channel_id=1, replica_groups=mesh['req'=32,'rep'=4] {'req'}, dimensions={0}, use_global_device_ids=true | all-gather | bytes 540672 | tf_op jit(solution)/shard_map/all_gather | solution.py:201
  97.3 2.1 convolution_convert_fusion.3
  99.4 3.9 all-to-all-start
  103.3 0.7 compare_and_fusion.2
  104.0 0.7 compare_select_fusion.3
  104.6 1.4 fusion.156
  106.7 0.9 dynamic-update-slice
  107.6 16.5 %all-reduce = s32[128]{0:T(128)S(1)} all-reduce(s32[128]{0:T(128)S(1)} %dynamic-update-slice), channel_id=1, replica_groups=mesh['req'=32,'rep'=4] {'req'}, use_global_device_ids=true, to_apply=%add | all-reduce | flops 128 | bytes 1024
  124.1 1.0 scatter_custom_fusion
  126.2 0.7 slice_bitcast_fusion
  126.9 0.8 copy.233
  127.7 0.7 compare_select_fusion
  128.5 0.7 iota_compare_fusion
  129.2 0.9 copy.235
  130.0 2.8 fusion.46
  132.9 76.8 %all_gather.23 = bf16[128,2,2,2]{3,2,1,0:T(2,128)(2,1)S(1)} all-gather(bf16[4,2,2,2]{3,2,1,0:T(2,128)(2,1)S(1)} %copy.235), channel_id=1, replica_groups=mesh['req'=32,'rep'=4] {'req'}, dimensions={0}, use_global_device_ids=true | all-gather | bytes 2112 | tf_op jit(solution)/shard_map/all_gather | solution.py:203
  209.7 0.8 fusion.153
  210.5 75.0 %all_gather.22 = s32[128,2,2,2]{3,2,1,0:T(2,128)S(1)} all-gather(s32[4,2,2,2]{3,2,1,0:T(2,128)S(1)} %copy.233), channel_id=1, replica_groups=mesh['req'=32,'rep'=4] {'req'}, dimensions={0}, use_global_device_ids=true | all-gather | bytes 4224 | tf_op jit(solution)/shard_map/all_gather | solution.py:202
  285.6 0.8 fusion.152
  286.4 82.6 %all_gather.25 = bf16[128,1,2048]{2,1,0:T(2,128)(2,1)S(1)} all-gather(bf16[4,1,2048]{2,1,0:T(2,128)(2,1)S(1)} %copy.241), channel_id=1, replica_groups=mesh['req'=32,'rep'=4] {'req'}, dimensions={0}, use_global_device_ids=true | all-gather | bytes 540672 | tf_op jit(solution)/shard_map/all_gather | solution.py:209
  370.8 2.9 fusion.49
  373.7 25.4 %gather_fusion = bf16[256,16,2,512]{3,2,1,0:T(2,128)(2,1)} fusion(bf16[256,16,2,512]{3,2,1,0:T(2,128)(2,1)} %param.26, s32[1024]{0:T(1024)S(1)} %pad_clamp_fusion.3), kind=kCustom, calls=%fused_computation.2 | custom fusion | bytes 16778240 | tf_op jit(solution)/shard_map/gather | solution.py:91
  399.1 14.0 reshape.554
  413.1 8.1 fusion.151
  421.2 0.7 gather_fusion.3
  421.9 0.7 broadcast_select_fusion
  422.6 0.7 select_reduce_fusion.1
  423.4 4.0 all-to-all-start.2
  427.8 8.1 all-to-all-done.2
  436.1 3.6 fusion.157
  439.7 1.3 fusion.158
  443.3 3.7 fusion.1
  447.1 1.4 fusion
  448.6 1.7 fusion.43
  450.3 0.8 copy.255
  451.7 3.9 all-to-all-start.3
  455.6 1.7 fusion.42
  457.2 0.8 copy.231
  458.0 0.6 copy.232
  458.7 5.5 all-to-all-done.3
  464.2 4.6 all-to-all-start.1
  469.4 1.3 gather_fusion.4
  470.7 6.6 all-to-all-done.1
  477.4 1.8 fusion.15
  479.2 1.9 fusion.13
  481.8 1.0 select_reduce_fusion
  482.9 388.7 %all-reduce.14.cloned.1.call-done = (bf16[128,1,2048]{2,0,1:T(8,128)(2,1)}, bf16[128,1,2048]{2,0,1:T(8,128)(2,1)}) async-done(((bf16[128,1,2048]{2,0,1:T(8,128)(2,1)}, bf16[128,1,2048]{2,0,1:T(8,128)(2,1)}), (bf16[128,1,2048]{2,0,1:T(8,128)(2,1)}, bf16[128,1,2048]{2,0,1:T(8,128)(2,1)})) %all-reduce.14.cloned.1.call-update) | async-done | bytes 1048592
  871.6 0.8 constant_dynamic-slice_fusion.3
  872.3 0.8 constant_dynamic-slice_fusion.1
  873.1 32.1 %all-reduce.8 = (bf16[4,1,2048]{2,0,1:T(4,128)(2,1)S(1)}, bf16[4,1,2048]{2,0,1:T(4,128)(2,1)S(1)}) all-reduce(bf16[4,1,2048]{2,0,1:T(4,128)(2,1)S(1)} %constant_dynamic-slice_fusion.3, bf16[4,1,2048]{2,0,1:T(4,128)(2,1)S(1)} %constant_dynamic-slice_fusion.1), channel_id=1, replica_groups=mesh['req'=32,'rep'=4] {'rep'}, use_global_device_ids=true, to_apply=%region_7.8 | all-reduce | flops 16384 | bytes 65536 | tf_op jit(solution)/shard_map/psum | solution.py:62
  905.5 87.1 %all_gather.27 = bf16[128,1,2048]{2,1,0:T(2,128)(2,1)S(1)} all-gather(bf16[4,1,2048]{2,1,0:T(2,128)(2,1)S(1)} %copy.258), channel_id=1, replica_groups=mesh['req'=32,'rep'=4] {'req'}, dimensions={0}, use_global_device_ids=true | all-gather | bytes 540672 | tf_op jit(solution)/shard_map/all_gather | solution.py:183
  992.7 79.9 %all_gather.24 = bf16[128,1,2048]{2,1,0:T(2,128)(2,1)S(1)} all-gather(bf16[4,1,2048]{2,1,0:T(2,128)(2,1)S(1)} %copy.237), channel_id=1, replica_groups=mesh['req'=32,'rep'=4] {'req'}, dimensions={0}, use_global_device_ids=true | all-gather | bytes 540672 | tf_op jit(solution)/shard_map/all_gather | solution.py:183
  1072.6 0.6 fusion.22
  1073.3 0.6 fusion.24
  1074.0 4.1 fusion.12
  1078.0 3.7 fusion.14
  1081.7 354.5 %all-reduce.12.cloned.1.call-done = (bf16[128,1,2048]{2,0,1:T(8,128)(2,1)}, bf16[128,1,2048]{2,0,1:T(8,128)(2,1)}) async-done(((bf16[128,1,2048]{2,0,1:T(8,128)(2,1)}, bf16[128,1,2048]{2,0,1:T(8,128)(2,1)}), (bf16[128,1,2048]{2,0,1:T(8,128)(2,1)}, bf16[128,1,2048]{2,0,1:T(8,128)(2,1)})) %all-reduce.12.cloned.1.call-update) | async-done | bytes 1048592
  1436.2 0.8 constant_dynamic-slice_fusion
  1437.0 0.8 constant_dynamic-slice_fusion.2
  1437.7 32.1 %all-reduce.7 = (bf16[4,1,2048]{2,0,1:T(4,128)(2,1)S(1)}, bf16[4,1,2048]{2,0,1:T(4,128)(2,1)S(1)}) all-reduce(bf16[4,1,2048]{2,0,1:T(4,128)(2,1)S(1)} %constant_dynamic-slice_fusion, bf16[4,1,2048]{2,0,1:T(4,128)(2,1)S(1)} %constant_dynamic-slice_fusion.2), channel_id=1, replica_groups=mesh['req'=32,'rep'=4] {'rep'}, use_global_device_ids=true, to_apply=%region_23.25 | all-reduce | flops 16384 | bytes 65536 | tf_op jit(solution)/shard_map/psum | solution.py:62
  1469.9 0.6 copy.261
  (98 shorter events, 7.9 us)
Async XLA Ops:
  6.5 1067.4 %copy-start = (bf16[1,352,2048]{2,1,0:T(8,128)(2,1)S(1)}, bf16[1,352,2048]{2,1,0:T(8,128)(2,1)}, u32[]{:S(2)}) copy-start(bf16[1,352,2048]{2,1,0:T(8,128)(2,1)} %param.25) | copy-start | bytes 4325380
  99.4 324.0 %all-to-all-start = ((bf16[32,4,1,128]{3,1,2,0:T(4,128)(2,1)}), bf16[32,4,1,128]{3,1,2,0:T(4,128)(2,1)S(1)}, u32[]{:S(2)}, u32[]{:S(2)}) async-start(bf16[32,4,1,128]{3,1,2,0:T(4,128)(2,1)} %bitcast.8), calls=%async_computation | async-start | bytes 65536 | tf_op jit(solution)/shard_map/all_to_all | solution.py:130
  129.2 240.1 %copy-start.8 = (bf16[1,2048,128]{2,1,0:T(8,128)(2,1)S(1)}, bf16[1,2048,128]{2,1,0:T(8,128)(2,1)}, u32[]{:S(2)}) copy-start(bf16[1,2048,128]{2,1,0:T(8,128)(2,1)} %param.21) | copy-start | bytes 1572868
  370.8 65.1 %copy-start.14 = (s32[4,2]{1,0:T(4,128)}, s32[4,2]{1,0:T(4,128)S(1)}, u32[]{:S(2)}) copy-start(s32[4,2]{1,0:T(4,128)S(1)} %broadcast_select_fusion.1) | copy-start | bytes 100
  423.4 16.4 %copy-start.13 = (s32[4,2]{1,0:T(4,128)}, s32[4,2]{1,0:T(4,128)S(1)}, u32[]{:S(2)}) copy-start(s32[4,2]{1,0:T(4,128)S(1)} %copy.216) | copy-start | bytes 100
  423.4 25.2 %copy-start.10 = (bf16[4,1,2,4,128]{4,1,3,0,2:T(2,128)(2,1)}, bf16[4,1,2,4,128]{4,1,3,0,2:T(2,128)(2,1)S(1)}, u32[]{:S(2)}) copy-start(bf16[4,1,2,4,128]{4,1,3,0,2:T(2,128)(2,1)S(1)} %stack.20) | copy-start | bytes 24580
  423.4 17.6 %copy-start.11 = (bf16[4,1,2,4,128]{4,1,3,0,2:T(2,128)(2,1)}, bf16[4,1,2,4,128]{4,1,3,0,2:T(2,128)(2,1)S(1)}, u32[]{:S(2)}) copy-start(bf16[4,1,2,4,128]{4,1,3,0,2:T(2,128)(2,1)S(1)} %stack.19) | copy-start | bytes 24580
  423.4 12.5 all-to-all-start.2
  435.9 3.8 copy-start.6
  439.7 2.1 copy-start.12
  443.3 3.7 copy-start.5
  447.1 1.5 copy-start.15
  447.1 30.3 %copy-start.7 = (bf16[1,128,2048]{2,1,0:T(8,128)(2,1)S(1)}, bf16[1,128,2048]{2,1,0:T(8,128)(2,1)}, u32[]{:S(2)}) copy-start(bf16[1,128,2048]{2,1,0:T(8,128)(2,1)} %param.22) | copy-start | bytes 1572868
  448.5 34.4 %copy-start.9 = (bf16[4,2,2048]{2,1,0:T(2,128)(2,1)S(1)}, bf16[4,2,2048]{2,1,0:T(2,128)(2,1)}, u32[]{:S(2)}) copy-start(bf16[4,2,2048]{2,1,0:T(2,128)(2,1)} %param.18) | copy-start | bytes 98308
  448.5 624.1 %copy-start.1 = (bf16[1,2048,352]{1,2,0:T(8,128)(2,1)S(1)}, bf16[1,2048,352]{1,2,0:T(8,128)(2,1)}, u32[]{:S(2)}) copy-start(bf16[1,2048,352]{1,2,0:T(8,128)(2,1)} %param.23) | copy-start | bytes 4325380
  451.7 12.5 all-to-all-start.3
  464.2 13.2 all-to-all-start.1
  468.8 402.8 %all-reduce.14.cloned.1.call-start = ((), (), s32[]{:S(2)}) async-start(), calls=%async_computation.5 | async-start | bytes 2097152
  481.2 955.0 %all-reduce.12.cloned.1.call-start = ((), (), s32[]{:S(2)}) async-start(), calls=%async_computation.4 | async-start | bytes 2097152
  992.7 81.3 %copy-start.4 = (bf16[128,1,2048]{2,1,0:T(2,128)(2,1)}, bf16[128,1,2048]{2,1,0:T(2,128)(2,1)S(1)}, u32[]{:S(2)}) copy-start(bf16[128,1,2048]{2,1,0:T(2,128)(2,1)S(1)} %all_gather.27) | copy-start | bytes 1572868
  1072.6 1.3 copy-start.2
  1073.9 4.1 copy-start.3
Sparse Core Ops, SparseCore 0:
  481.3 390.2 all-reduce.13
  1081.8 354.3 all-reduce.11
where the time goes:
time: 1480 us
  waiting for transfers between devices  763 us (52%)
  blocking collectives  570 us (39%)
  local copies, waits for them, and re-layouts  67.3 us (5%)
  matrix products  35 us (2%)
  starting transfers between devices  16.4 us (1%)
  between operations  15.1 us (1%)
    unnamed x4, waiting for transfers between devices  743 us
    all_gather x2, blocking collectives, section(): block_rows = lax.all_gather(hidden_normed, 'req', axis=0, tiled=True)  167 us
    all_gather x1, blocking collectives, shards(): lax.all_gather(normed[:, 0:1], 'req', axis=0, tiled=True)  88.1 us
    all_gather x1, blocking collectives, shards(): second_rows = lax.all_gather(normed[:, 1:2], 'req', axis=0, tiled=True)  82.6 us
    all_gather x1, blocking collectives, shards(): lax.all_gather(route_gates, 'req', axis=0, tiled=True)  76.8 us
    all_gather x1, blocking collectives, shards(): lax.all_gather(route_ids, 'req', axis=0, tiled=True)  75 us
    psum x2, blocking collectives, combine(): return lax.psum(partial_value, 'rep').astype(jnp.float32)  64.1 us
  transfers between devices with their start and end apart: 6, of which 5 were waited for; matrix products, arithmetic and copies ran while one was open for 5% of the time, Pallas kernels for 0%

commit v1 on v0

v1 whole, which is shorter than its diff:
```python
import math

import jax
import jax.numpy as jnp
from jax import lax
from jax.sharding import PartitionSpec as P

HD = 128
EXPERTS = 8
EPSILON = 1e-06
MASKED = -1e30
F32 = jnp.float32
BF16 = jnp.bfloat16


def dot(a, b):
    return jnp.dot(a, b, preferred_element_type=F32)


def attend(queries, cache_keys, cache_values, lengths, extra_keys, extra_values, extra_live):
    inv_scale = 1.0 / math.sqrt(queries.shape[-1])
    cache_scores = (
        jnp.einsum("jskhc,jlhc->jskhl", queries, cache_keys, preferred_element_type=F32)
        * inv_scale
    )
    alive_mask = jnp.arange(cache_keys.shape[1], dtype=jnp.int32)[None, :] < lengths[:, None]
    cache_scores = jnp.where(alive_mask[:, None, None, None, :], cache_scores, MASKED)
    extra_scores = (
        jnp.einsum("jskhc,jxhc->jskhx", queries, extra_keys, preferred_element_type=F32)
        * inv_scale
    )
    extra_scores = jnp.where(extra_live[None, :, None, None, :], extra_scores, MASKED)
    highest = jnp.maximum(jnp.max(cache_scores, axis=-1), jnp.max(extra_scores, axis=-1))[..., None]
    cache_exp = jnp.exp(cache_scores - highest)
    extra_exp = jnp.exp(extra_scores - highest)
    denominator = (jnp.sum(cache_exp, axis=-1) + jnp.sum(extra_exp, axis=-1))[..., None]
    cache_weight = (cache_exp / denominator).astype(BF16)
    extra_weight = (extra_exp / denominator).astype(BF16)
    mixture = jnp.einsum("jskhl,jlhc->jskhc", cache_weight, cache_values, preferred_element_type=F32)
    mixture = mixture + jnp.einsum(
        "jskhx,jxhc->jskhc", extra_weight, extra_values, preferred_element_type=F32
    )
    return mixture.astype(BF16)


def shards(
    tokens,
    norm_gains,
    w_kv,
    w_query,
    w_out,
    w_gate,
    w_up,
    w_down,
    kv_pages,
    page_table,
    cache_len,
    route_ids,
    route_gates,
    new_slot,
):
    req_count = lax.axis_size("req")
    rep_count = lax.axis_size("rep")
    mine = tokens.shape[0]
    width = tokens.shape[-1]
    rows = 2 * mine
    total = rows * req_count
    holders = req_count // EXPERTS
    half = width // 2
    quarter = width // rep_count
    heads_rep = kv_pages.shape[-1] // HD
    rank = lax.axis_index("req")
    rep = lax.axis_index("rep")
    core = rep % 2
    swap = [(p, p ^ 1) for p in range(rep_count)]
    wide_groups = [
        [r * rep_count + 2 * z + c for r in range(req_count) for z in range(rep_count // 2)]
        for c in range(2)
    ]
    peers = req_count * rep_count // 2

    def spread_req(value):
        return lax.all_to_all(value, "req", split_axis=0, concat_axis=0, tiled=True)

    def spread_wide(value):
        return lax.all_to_all(
            value,
            ("req", "rep"),
            split_axis=0,
            concat_axis=0,
            tiled=True,
            axis_index_groups=wide_groups,
        )

    def other_core(value):
        return lax.ppermute(value, "rep", swap)

    def pick(value, index, axis):
        return lax.dynamic_index_in_dim(value, index, axis, keepdims=False)

    inputs = tokens.astype(F32).transpose(1, 0, 2).reshape(rows, width)
    scaling = lax.rsqrt(jnp.mean(inputs * inputs, axis=-1, keepdims=True) + EPSILON)
    normed = (inputs * scaling * norm_gains[0]).astype(BF16)
    own_pos = rank * rows + jnp.arange(mine, dtype=jnp.int32)
    moved_pos = (new_slot // mine) * rows + mine + new_slot % mine
    source = jnp.concatenate([own_pos, moved_pos])
    ids = route_ids.transpose(1, 2, 0, 3).reshape(2, rows, 2)
    gates = route_gates.astype(F32).transpose(1, 2, 0, 3).reshape(2, rows, 2)
    experts_row = jnp.arange(EXPERTS, dtype=jnp.int32)
    shares = jnp.sum(jnp.where(ids[..., None] == experts_row, gates[..., None], 0.0), axis=2)

    extras = jnp.concatenate([source[:, None], ids[0]], axis=1).astype(BF16)
    extras = jnp.pad(extras, ((0, 0), (0, HD - extras.shape[1])))
    message = jnp.concatenate(
        [lax.dynamic_slice_in_dim(normed, core * half, half, 1), extras], axis=1
    )
    gathered = spread_req(jnp.broadcast_to(message[None], (req_count,) + message.shape))
    gathered = gathered.reshape(total, half + HD)
    near, notes = gathered[:, :half], gathered[:, half:]
    far = other_core(near)

    wq = w_query[0].reshape(2, half, HD)
    queries = (dot(near, pick(wq, core, 0)) + dot(far, pick(wq, 1 - core, 0))).astype(BF16)
    order = (
        notes[:, :1].astype(jnp.int32) == jnp.arange(total, dtype=jnp.int32)[None, :]
    ).astype(BF16)
    ordered = dot(order, queries).astype(BF16)
    arrived = spread_req(ordered.reshape(req_count, rows, HD))

    own_order = lax.dynamic_slice_in_dim(order, rank * rows, rows, 0)
    own_ids = dot(own_order, notes)[:, 1:3].astype(jnp.int32)
    wkv = w_kv.reshape(2, half, 2 * heads_rep * HD)
    fresh = (
        dot(dot(own_order, near).astype(BF16), pick(wkv, core, 0))
        + dot(dot(own_order, far).astype(BF16), pick(wkv, 1 - core, 0))
    ).astype(BF16)
    extra = fresh.reshape(2, mine, 2, heads_rep, HD).transpose(1, 0, 2, 3, 4)

    chosen = (own_ids.reshape(2, mine, 2)[..., None] == experts_row).astype(BF16)
    arrived = arrived.reshape(EXPERTS, holders, 2, mine, HD)
    picked = jnp.einsum("sjke,ehsjc->jskhc", chosen, arrived, preferred_element_type=F32).astype(BF16)
    pages = kv_pages[page_table].reshape(mine, -1, 2, heads_rep, HD)
    extra_live = jnp.array([[True, False], [True, True]])
    result = attend(
        picked, pages[:, :, 0], pages[:, :, 1], cache_len, extra[:, :, 0], extra[:, :, 1], extra_live
    )
    back = jnp.einsum("sjke,jskhc->ehsjc", chosen, result, preferred_element_type=F32).astype(BF16)
    returned = spread_req(back.reshape(req_count, rows, HD)).reshape(total, HD)
    answers = lax.dot_general(
        order, returned, (((0,), (0,)), ((), ())), preferred_element_type=F32
    ).astype(BF16)

    def reduce_wide(partial, share):
        parts = partial.reshape(total, rep_count // 2, 2, quarter)
        theirs = other_core(pick(parts, 1 - core, 2).astype(BF16))
        summed = (pick(parts, core, 2) + theirs.astype(F32)).astype(BF16)
        summed = summed.reshape(req_count, rows, rep_count // 2, quarter).transpose(0, 2, 1, 3)
        got = spread_wide(summed.reshape(peers, rows, quarter))
        got = got.reshape(EXPERTS, peers // EXPERTS, rows, quarter).astype(F32)
        return jnp.sum(jnp.sum(got, axis=1) * share.T[:, :, None], axis=0)

    hidden = lax.dynamic_slice_in_dim(inputs, rep * quarter, quarter, 1) + reduce_wide(
        dot(answers, w_out[0]), shares[0]
    )
    block = spread_wide(jnp.broadcast_to(hidden.astype(BF16)[None], (peers, rows, quarter)))
    near = block.reshape(req_count, rep_count // 2, rows, quarter)
    far = other_core(near)
    near32, far32 = near.astype(F32), far.astype(F32)
    squares = jnp.sum(near32 * near32, axis=(1, 3)) + jnp.sum(far32 * far32, axis=(1, 3))
    scaling = lax.rsqrt(squares / width + EPSILON)[:, None, :, None]
    gain = norm_gains[1].reshape(rep_count // 2, 2, quarter)
    near_n = (near32 * scaling * pick(gain, core, 1)[None, :, None, :]).astype(BF16)
    far_n = (far32 * scaling * pick(gain, 1 - core, 1)[None, :, None, :]).astype(BF16)

    def project(weight):
        split = weight.reshape(rep_count // 2, 2, quarter, -1)
        return jnp.einsum(
            "rzbc,zcf->rbf", near_n, pick(split, core, 1), preferred_element_type=F32
        ) + jnp.einsum("rzbc,zcf->rbf", far_n, pick(split, 1 - core, 1), preferred_element_type=F32)

    units = (jax.nn.silu(project(w_gate[0])) * project(w_up[0])).astype(BF16)
    feed = reduce_wide(dot(units.reshape(total, -1), w_down[0]), shares[1])
    final = lax.all_gather((hidden + feed).astype(BF16), "rep", axis=1, tiled=True)
    return final.reshape(2, mine, width).transpose(1, 0, 2)


def solution(mesh):
    in_specs = (
        P("req", None, None),
        P(),
        P(None, None, "rep"),
        P("req", None, "rep"),
        P("req", "rep", None),
        P("req", None, "rep"),
        P("req", None, "rep"),
        P("req", "rep", None),
        P("req", None, None, "rep"),
        P("req", None),
        P("req"),
        P("req", None, None, None),
        P("req", None, None, None),
        P("req"),
    )
    out_specs = P("req", None, None)
    return jax.shard_map(shards, mesh=mesh, in_specs=in_specs, out_specs=out_specs, check_vma=False)
```

time: 1480 us -> 210 us (0.14)
  waiting for transfers between devices: 763 us -> 41.7 us
  blocking collectives: 570 us -> 6.99 us
  starting transfers between devices: 16.4 us -> 50.1 us
    unnamed x4 -> x0, waiting for transfers between devices: 743 us -> none
    all_gather x6 -> x1, blocking collectives: 490 us -> 6.99 us  [shards(): lax.all_gather((hidden + feed).astype(BF16), 'rep', axis=1, tiled=True)]
    psum x2 -> x0, blocking collectives: 64.1 us -> none  [combine(): return lax.psum(partial_value, 'rep').astype(jnp.float32)]
    all_to_all x4 -> x6, starting transfers between devices: 16.3 us -> 43.1 us  [the longest x3 25.5 us: spread_req(): return lax.all_to_all(value, 'req', split_axis=0, concat_axis=0, tiled=True)]
    all_to_all x4 -> x6, waiting for transfers between devices: 20.3 us -> 37.6 us  [the longest x3 24.9 us: spread_wide(): lax.all_to_all(value, ('req', 'rep'), split_axis=0, concat_axis=0, tiled=...]
    unnamed x1 -> x0, blocking collectives: 16.5 us -> none
  transfers between devices with their start and end apart: 6 -> 10, of which waited for: 5 -> 8; matrix products, arithmetic and copies ran while one was open for 5% -> 38% of each run, Pallas kernels for 0% -> 0%
where the time goes in v1:
time: 210 us; the launch traced here: 208 us
  local copies, waits for them, and re-layouts  80.6 us (38%)
  starting transfers between devices  50.1 us (24%)
  waiting for transfers between devices  41.7 us (20%)
  matrix products  20.5 us (10%)
  other arithmetic  7.68 us (4%)
  blocking collectives  6.99 us (3%)
    all_to_all x3, starting transfers between devices, spread_req(): return lax.all_to_all(value, 'req', split_axis=0, concat_axis=0, tiled=True)  25.5 us
    gather x1, local copies, waits for them, and re-layouts, shards(): pages = kv_pages[page_table].reshape(mine, -1, 2, heads_rep, HD)  25.4 us
    all_to_all x3, waiting for transfers between devices, spread_wide(): lax.all_to_all(value, ('req', 'rep'), split_axis=0, concat_axis=0, tiled=...  24.9 us
    all_to_all x3, starting transfers between devices, spread_wide(): lax.all_to_all(value, ('req', 'rep'), split_axis=0, concat_axis=0, tiled=...  17.6 us
    reshape x1, local copies, waits for them, and re-layouts, shards(): pages = kv_pages[page_table].reshape(mine, -1, 2, heads_rep, HD)  14 us
    all_to_all x3, waiting for transfers between devices, spread_req(): return lax.all_to_all(value, 'req', split_axis=0, concat_axis=0, tiled=True)  12.8 us
    dot_general x7, matrix products, dot(): return jnp.dot(a, b, preferred_element_type=F32)  10.3 us
    slice x1, local copies, waits for them, and re-layouts, shards(): pages[:, :, 0]  8.1 us
  transfers between devices with their start and end apart: 10, of which 8 were waited for; matrix products, arithmetic and copies ran while one was open for 38% of the time, Pallas kernels for 0%

profile of v1, /device:TPU:1, one launch (start us, length us, event | category | flops | bytes accessed | tf_op | source)
XLA Modules:
  0.0 208.1 jit_solution(593229244618823262)
XLA Ops:
  0.0 0.9 convert_bitcast_fusion
  0.9 0.9 multiply_reduce_fusion.3
  1.7 0.8 slice_reduce_fusion
  2.8 0.7 fusion.86
  3.6 0.1 copy.199
  3.7 0.7 slice_convert_fusion
  4.4 0.1 copy.241
  4.7 0.9 broadcast_in_dim.76
  5.5 11.2 %all-to-all-start = ((bf16[32,8,1152]{2,1,0:T(8,128)(2,1)}), bf16[32,8,1152]{2,1,0:T(8,128)(2,1)S(1)}, u32[]{:S(2)}, u32[]{:S(2)}) async-start(bf16[32,8,1152]{2,1,0:T(8,128)(2,1)} %broadcast_in_dim.76), calls=%async_computation | async-start | bytes 1179648 | tf_op jit(solution)/shard_map/all_to_all | solution.py:83
  16.8 25.4 %gather_fusion = bf16[256,16,2,512]{3,2,1,0:T(2,128)(2,1)} fusion(bf16[256,16,2,512]{3,2,1,0:T(2,128)(2,1)} %param.23, s32[1024]{0:T(1024)S(1)} %pad_clamp_fusion), kind=kCustom, calls=%fused_computation | custom fusion | bytes 16778240 | tf_op jit(solution)/shard_map/gather | solution.py:142
  42.2 14.0 %reshape.175 = bf16[4,1024,2,4,128]{4,3,2,1,0:T(4,128)(2,1)} reshape(bf16[256,16,2,512]{3,2,1,0:T(2,128)(2,1)} %gather_fusion) | data formatting | bytes 16777216 | tf_op jit(solution)/shard_map/reshape | solution.py:142
  56.2 8.1 %fusion.91 = (bf16[4,1024,1,4,128]{4,3,2,1,0:T(4,128)(2,1)}, bf16[4,1024,1,4,128]{4,3,2,1,0:T(4,128)(2,1)}) fusion(bf16[4,1024,2,4,128]{4,3,2,1,0:T(4,128)(2,1)} %reshape.175), kind=kLoop, calls=%fused_computation.151 | loop fusion | bytes 16777216 | tf_op jit(solution)/shard_map/slice | solution.py:145
  64.3 7.7 %reshape.133 = bf16[2,1024,1024]{2,1,0:T(8,128)(2,1)} reshape(bf16[2048,2,512]{2,1,0:T(2,128)(2,1)} %param.17) | data formatting | bytes 8388608 | tf_op jit(solution)/shard_map/reshape | solution.py:132
  72.2 0.1 convert_reduce_fusion.2
  72.3 1.0 collective-permute-start
  73.3 0.1 iota_compare_fusion
  73.5 0.2 convolution_convert_fusion.6
  73.8 0.3 fusion.50
  74.1 0.8 collective-permute-done
  74.9 1.1 fusion.14
  76.0 9.5 %all-to-all-start.1 = ((bf16[32,8,128]{2,1,0:T(8,128)(2,1)}), bf16[32,8,128]{2,1,0:T(8,128)(2,1)S(1)}, u32[]{:S(2)}, u32[]{:S(2)}) async-start(bf16[32,8,128]{2,1,0:T(8,128)(2,1)} %fusion.14), calls=%async_computation.1 | async-start | bytes 131072 | tf_op jit(solution)/shard_map/all_to_all | solution.py:83
  85.5 2.1 %fusion.2 = f32[8,1024]{1,0:T(8,128)S(1)} fusion(bf16[2,1024,1024]{2,1,0:T(8,128)(2,1)} %reshape.133, s32[]{:T(128)S(6)} %select_n.76, bf16[256,1024]{1,0:T(8,128)(2,1)S(1)} %collective-permute-done, pred[256,256]{1,0:T(8,128)(4,1)S(1)} %iota_compare_fusion, s32[]{:T(128)S(6)} %select_n.74), kind=kOutput, calls=%fused_computation.5 | convolution fusion | flops 20979712 | bytes 2656264 | tf_op jit(solution)/shard_map/dot_general | solution.py:17
  87.6 2.1 %fusion.23 = bf16[8,1024]{1,0:T(8,128)(2,1)S(1)} fusion(f32[8,1024]{1,0:T(8,128)S(1)} %fusion.2, bf16[2,1024,1024]{2,1,0:T(8,128)(2,1)} %reshape.133, s32[]{:T(128)S(6)} %select_n.75, pred[256,256]{1,0:T(8,128)(4,1)S(1)} %iota_compare_fusion, s32[]{:T(128)S(6)} %select_n.74, bf16[256,1152]{1,0:T(8,128)(2,1)S(1)} %bitcast.223), kind=kOutput, calls=%fused_computation.38 | convolution fusion | flops 20996096 | bytes 2672648 | tf_op jit(solution)/shard_map/dot_general | solution.py:17
  89.8 4.4 %all-to-all-done.1 = bf16[32,8,128]{2,1,0:T(8,128)(2,1)S(1)} async-done(((bf16[32,8,128]{2,1,0:T(8,128)(2,1)}), bf16[32,8,128]{2,1,0:T(8,128)(2,1)S(1)}, u32[]{:S(2)}, u32[]{:S(2)}) %all-to-all-start.1) | async-done | bytes 65568 | tf_op jit(solution)/shard_map/all_to_all | solution.py:83
  94.2 0.2 convolution_convert_fusion.5
  94.4 3.6 %fusion.92 = (f32[4,2,2,4]{2,1,3,0:T(2,128)S(1)}, f32[4,2,2,4,1024]{4,2,1,3,0:T(2,128)S(1)}) fusion(bf16[4,2,2,4,128]{4,2,3,1,0:T(2,128)(2,1)S(1)} %convolution_convert_fusion.5, bf16[4,1024,1,4,128]{4,3,2,1,0:T(4,128)(2,1)} %get-tuple-element.5, pred[4,1024]{1,0:T(4,128)(4,1)S(1)} %iota_compare_fusion.5), kind=kOutput, calls=%fused_computation.152 | convolution fusion | flops 16973760 | bytes 4477184 | tf_op jit(solution)/shard_map/jskhc,jlhc->jskhl/dot_general | solution.py:23
  98.0 0.4 fusion.93
  98.6 0.3 fusion.56
  98.9 0.8 fusion.1
  99.7 0.4 fusion.16
  100.1 0.7 copy.212
  100.7 4.8 %all-to-all-start.2 = ((bf16[32,8,128]{2,1,0:T(8,128)(2,1)}), bf16[32,8,128]{2,1,0:T(8,128)(2,1)S(1)}, u32[]{:S(2)}, u32[]{:S(2)}) async-start(bf16[32,8,128]{2,1,0:T(8,128)(2,1)} %bitcast.32), calls=%async_computation.2 | async-start | bytes 131072 | tf_op jit(solution)/shard_map/all_to_all | solution.py:83
  105.6 0.3 copy.249
  105.9 8.3 %all-to-all-done.2 = bf16[32,8,128]{2,1,0:T(8,128)(2,1)S(1)} async-done(((bf16[32,8,128]{2,1,0:T(8,128)(2,1)}), bf16[32,8,128]{2,1,0:T(8,128)(2,1)S(1)}, u32[]{:S(2)}, u32[]{:S(2)}) %all-to-all-start.2) | async-done | bytes 65568 | tf_op jit(solution)/shard_map/all_to_all | solution.py:83
  114.2 0.7 fusion.34
  115.0 2.6 %collective-permute-start.1 = (bf16[256,2,512]{2,0,1:T(8,128)(2,1)S(1)}, bf16[256,2,512]{2,0,1:T(8,128)(2,1)S(1)}, u32[]{:S(2)}, u32[]{:S(2)}) collective-permute-start(bf16[256,2,512]{2,0,1:T(8,128)(2,1)S(1)} %fusion.35), channel_id=1, source_target_pairs={{0,1},{1,0},{2,3},{3,2},{4,5},{5,4},{6,7},{7,6},{8,9},{9,8},{10,11... | collective-permute-start | bytes 1572872 | tf_op jit(solution)/shard_map/ppermute | solution.py:96
  117.7 1.4 collective-permute-done.1
  119.1 0.2 fusion.37
  119.3 0.9 copy.214
  120.2 4.6 %all-to-all-start.3 = ((bf16[64,8,512]{2,1,0:T(8,128)(2,1)}), bf16[64,8,512]{2,1,0:T(8,128)(2,1)S(1)}, u32[]{:S(2)}, u32[]{:S(2)}) async-start(bf16[64,8,512]{2,1,0:T(8,128)(2,1)} %bitcast.43), calls=%async_computation.3 | async-start | bytes 1048576 | tf_op jit(solution)/shard_map/all_to_all | solution.py:86
  125.1 11.7 %all-to-all-done.3 = bf16[64,8,512]{2,1,0:T(8,128)(2,1)S(1)} async-done(((bf16[64,8,512]{2,1,0:T(8,128)(2,1)}), bf16[64,8,512]{2,1,0:T(8,128)(2,1)S(1)}, u32[]{:S(2)}, u32[]{:S(2)}) %all-to-all-start.3) | async-done | bytes 524320 | tf_op jit(solution)/shard_map/all_to_all | solution.py:86
  137.0 0.8 broadcast_in_dim.86
  137.8 4.9 %all-to-all-start.4 = ((bf16[64,8,512]{2,1,0:T(8,128)(2,1)}), bf16[64,8,512]{2,1,0:T(8,128)(2,1)S(1)}, u32[]{:S(2)}, u32[]{:S(2)}) async-start(bf16[64,8,512]{2,1,0:T(8,128)(2,1)} %broadcast_in_dim.86), calls=%async_computation.4 | async-start | bytes 1048576 | tf_op jit(solution)/shard_map/all_to_all | solution.py:86
  142.7 1.1 reshape_squeeze.14
  143.8 3.8 %reshape_squeeze.15 = bf16[2,2,512,352]{2,1,0,3:T(2,128)(2,1)S(1)} reshape(bf16[1,2048,352]{1,2,0:T(8,128)(2,1)} %param.21) | data formatting | bytes 2883584 | tf_op jit(solution)/shard_map/reshape;squeeze | solution.py:176
  147.6 4.7 %dot_general.94 = bf16[2,2,512,352]{2,1,0,3:T(2,128)(2,1)} reshape(bf16[2048,352]{0,1:T(8,128)(2,1)} %bitcast.228) | data formatting | bytes 2883584 | tf_op jit(solution)/shard_map/dot_general | solution.py:17
  152.3 1.2 all-to-all-done.4
  153.5 3.2 %collective-permute-start.2 = (bf16[32,2,8,512]{3,2,1,0:T(8,128)(2,1)S(1)}, bf16[32,2,8,512]{3,2,1,0:T(8,128)(2,1)}, u32[]{:S(2)}, u32[]{:S(2)}) collective-permute-start(bf16[32,2,8,512]{3,2,1,0:T(8,128)(2,1)S(1)} %bitcast.225), channel_id=1, source_target_pairs={{0,1},{1,0},{2,3},{3,2},{4,5},{5,4},{6,7},{7,6},{8,9},{9,8},{10,11... | collective-permute-start | bytes 1572872 | tf_op jit(solution)/shard_map/ppermute | solution.py:96
  156.7 7.3 %constant_dynamic-slice_fusion = (bf16[2,1,512,352]{2,1,0,3:T(2,128)(2,1)}, bf16[2,1,512,352]{2,1,0,3:T(2,128)(2,1)}, bf16[2,1,512,352]{2,1,0,3:T(2,128)(2,1)}, bf16[2,1,512,352]{2,1,0,3:T(2,128)(2,1)}) fusion(bf16[2,2,512,352]{2,1,0,3:T(2,128)(2,1)S(1)} %reshape_squeeze.15, s32[]{:T(128)S(6)} %select_n.76, s32[]{:T(128)S(6)} %select_n.75, ...), kind=kLoop, calls=%fused_computation.114 | loop fusion | bytes 5767176 | tf_op jit(solution)/shard_map/jit(dynamic_index_in_dim)/dynamic_slice | solution.py:99
  164.0 0.2 multiply_reduce_fusion
  164.3 1.4 fusion.27
  165.8 2.0 convolution_bitcast_fusion.3
  167.8 1.2 convolution_bitcast_fusion.1
  169.0 1.6 fusion.10
  170.7 3.8 %fusion.8 = f32[256,2,2,512]{3,0,2,1:T(8,128)} fusion(bf16[2,2,512,352]{2,1,0,3:T(2,128)(2,1)S(1)} %copy-done.7, f32[32,8,352]{2,1,0:T(8,128)} %convolution_bitcast_fusion.1, bf16[2,1,512,352]{2,1,0,3:T(2,128)(2,1)S(1)} %copy-done.3, bf16[32,2,8,512]{3,2,1,0:T(8,128)(2,1)} %collective-permute-done.2, f32[2,512]{1,0:T(2,128)S(1)} %get-tuple-element.25, ...), kind=kOutput, calls=%fused_computation.11 | convolution fusion | flops 555327488 | bytes 5510144 | tf_op jit(solution)/shard_map/dot_general | solution.py:17
  174.5 1.3 fusion.36
  175.8 0.1 collective-permute-start.3
  175.9 1.9 collective-permute-done.3
  177.8 1.4 fusion.38
  179.2 0.9 copy.227
  180.1 8.1 %all-to-all-start.5 = ((bf16[64,8,512]{2,1,0:T(8,128)(2,1)}), bf16[64,8,512]{2,1,0:T(8,128)(2,1)S(1)}, u32[]{:S(2)}, u32[]{:S(2)}) async-start(bf16[64,8,512]{2,1,0:T(8,128)(2,1)} %bitcast.74), calls=%async_computation.5 | async-start | bytes 1048576 | tf_op jit(solution)/shard_map/all_to_all | solution.py:86
  188.2 12.0 %all-to-all-done.5 = bf16[64,8,512]{2,1,0:T(8,128)(2,1)S(1)} async-done(((bf16[64,8,512]{2,1,0:T(8,128)(2,1)}), bf16[64,8,512]{2,1,0:T(8,128)(2,1)S(1)}, u32[]{:S(2)}, u32[]{:S(2)}) %all-to-all-start.5) | async-done | bytes 524320 | tf_op jit(solution)/shard_map/all_to_all | solution.py:86
  200.4 7.0 %all_gather.3 = bf16[8,2048]{1,0:T(8,128)(2,1)S(1)} all-gather(bf16[8,512]{1,0:T(8,128)(2,1)S(1)} %add_convert_fusion), channel_id=1, replica_groups=mesh['req'=32,'rep'=4] {'rep'}, dimensions={1}, use_global_device_ids=true | all-gather | bytes 40960 | tf_op jit(solution)/shard_map/all_gather | solution.py:183
  207.4 0.7 copy.229
  (76 shorter events, 2.1 us)
Async XLA Ops:
  0.0 73.8 %copy-start = (bf16[1,2048,128]{2,1,0:T(8,128)(2,1)S(1)}, bf16[1,2048,128]{2,1,0:T(8,128)(2,1)}, u32[]{:S(2)}) copy-start(bf16[1,2048,128]{2,1,0:T(8,128)(2,1)} %param.18) | copy-start | bytes 1572868
  0.0 16.7 %copy-start.11 = (s32[4,64]{1,0:T(4,128)S(1)}, s32[4,64]{1,0:T(4,128)}, u32[]{:S(2)}) copy-start(s32[4,64]{1,0:T(4,128)} %param.24) | copy-start | bytes 3076
  5.5 66.6 %all-to-all-start = ((bf16[32,8,1152]{2,1,0:T(8,128)(2,1)}), bf16[32,8,1152]{2,1,0:T(8,128)(2,1)S(1)}, u32[]{:S(2)}, u32[]{:S(2)}) async-start(bf16[32,8,1152]{2,1,0:T(8,128)(2,1)} %broadcast_in_dim.76), calls=%async_computation | async-start | bytes 1179648 | tf_op jit(solution)/shard_map/all_to_all | solution.py:83
  64.3 7.7 %copy-start.12 = (s32[4]{0:T(128)S(1)}, s32[4]{0:T(128)}, u32[]{:S(2)}) copy-start(s32[4]{0:T(128)} %param.25) | copy-start | bytes 52
  72.3 2.6 %collective-permute-start = (bf16[256,1024]{1,0:T(8,128)(2,1)S(1)}, bf16[256,1024]{1,0:T(8,128)(2,1)S(1)}, u32[]{:S(2)}, u32[]{:S(2)}) collective-permute-start(bf16[256,1024]{1,0:T(8,128)(2,1)S(1)} %slice.65), channel_id=1, source_target_pairs={{0,1},{1,0},{2,3},{3,2},{4,5},{5,4},{6,7},{7,6},{8,9},{9,8},{10,11... | collective-permute-start | bytes 1572872 | tf_op jit(solution)/shard_map/ppermute | solution.py:96
  76.0 18.1 %all-to-all-start.1 = ((bf16[32,8,128]{2,1,0:T(8,128)(2,1)}), bf16[32,8,128]{2,1,0:T(8,128)(2,1)S(1)}, u32[]{:S(2)}, u32[]{:S(2)}) async-start(bf16[32,8,128]{2,1,0:T(8,128)(2,1)} %fusion.14), calls=%async_computation.1 | async-start | bytes 131072 | tf_op jit(solution)/shard_map/all_to_all | solution.py:83
  94.4 3.7 %copy-start.13 = (pred[2,2]{1,0:T(4,128)(4,1)S(1)}, pred[2,2]{1,0:T(4,128)(4,1)}, u32[]{:S(2)}) copy-start(pred[2,2]{1,0:T(4,128)(4,1)} %constant.126.clone) | copy-start | bytes 16
  94.4 4.5 %copy-start.2 = (bf16[4,1024,1,4,128]{4,3,2,1,0:T(4,128)(2,1)S(1)}, bf16[4,1024,1,4,128]{4,3,2,1,0:T(4,128)(2,1)}, u32[]{:S(2)}) copy-start(bf16[4,1024,1,4,128]{4,3,2,1,0:T(4,128)(2,1)} %get-tuple-element.6) | copy-start | bytes 12582916
  98.9 6.7 %copy-start.8 = (bf16[1,128,2048]{2,1,0:T(8,128)(2,1)S(1)}, bf16[1,128,2048]{2,1,0:T(8,128)(2,1)}, u32[]{:S(2)}) copy-start(bf16[1,128,2048]{2,1,0:T(8,128)(2,1)} %param.19) | copy-start | bytes 1572868
  100.7 13.5 %all-to-all-start.2 = ((bf16[32,8,128]{2,1,0:T(8,128)(2,1)}), bf16[32,8,128]{2,1,0:T(8,128)(2,1)S(1)}, u32[]{:S(2)}, u32[]{:S(2)}) async-start(bf16[32,8,128]{2,1,0:T(8,128)(2,1)} %bitcast.32), calls=%async_computation.2 | async-start | bytes 131072 | tf_op jit(solution)/shard_map/all_to_all | solution.py:83
  105.9 11.7 %copy-start.9 = (s32[4,2,2,2]{0,3,2,1:T(2,128)S(1)}, s32[4,2,2,2]{0,3,2,1:T(2,128)}, u32[]{:S(2)}) copy-start(s32[4,2,2,2]{0,3,2,1:T(2,128)} %param.26) | copy-start | bytes 388
  115.0 4.1 %collective-permute-start.1 = (bf16[256,2,512]{2,0,1:T(8,128)(2,1)S(1)}, bf16[256,2,512]{2,0,1:T(8,128)(2,1)S(1)}, u32[]{:S(2)}, u32[]{:S(2)}) collective-permute-start(bf16[256,2,512]{2,0,1:T(8,128)(2,1)S(1)} %fusion.35), channel_id=1, source_target_pairs={{0,1},{1,0},{2,3},{3,2},{4,5},{5,4},{6,7},{7,6},{8,9},{9,8},{10,11... | collective-permute-start | bytes 1572872 | tf_op jit(solution)/shard_map/ppermute | solution.py:96
  117.7 7.1 %copy-start.10 = (bf16[4,2,2,2]{0,3,2,1:T(2,128)(2,1)S(1)}, bf16[4,2,2,2]{0,3,2,1:T(2,128)(2,1)}, u32[]{:S(2)}) copy-start(bf16[4,2,2,2]{0,3,2,1:T(2,128)(2,1)} %param.27) | copy-start | bytes 196
  119.3 23.4 %copy-start.6 = (bf16[1,2048,352]{1,2,0:T(8,128)(2,1)S(1)}, bf16[1,2048,352]{1,2,0:T(8,128)(2,1)}, u32[]{:S(2)}) copy-start(bf16[1,2048,352]{1,2,0:T(8,128)(2,1)} %param.20) | copy-start | bytes 4325380
  120.2 16.6 %all-to-all-start.3 = ((bf16[64,8,512]{2,1,0:T(8,128)(2,1)}), bf16[64,8,512]{2,1,0:T(8,128)(2,1)S(1)}, u32[]{:S(2)}, u32[]{:S(2)}) async-start(bf16[64,8,512]{2,1,0:T(8,128)(2,1)} %bitcast.43), calls=%async_computation.3 | async-start | bytes 1048576 | tf_op jit(solution)/shard_map/all_to_all | solution.py:86
  137.8 15.7 %all-to-all-start.4 = ((bf16[64,8,512]{2,1,0:T(8,128)(2,1)}), bf16[64,8,512]{2,1,0:T(8,128)(2,1)S(1)}, u32[]{:S(2)}, u32[]{:S(2)}) async-start(bf16[64,8,512]{2,1,0:T(8,128)(2,1)} %broadcast_in_dim.86), calls=%async_computation.4 | async-start | bytes 1048576 | tf_op jit(solution)/shard_map/all_to_all | solution.py:86
  153.5 10.8 %collective-permute-start.2 = (bf16[32,2,8,512]{3,2,1,0:T(8,128)(2,1)S(1)}, bf16[32,2,8,512]{3,2,1,0:T(8,128)(2,1)}, u32[]{:S(2)}, u32[]{:S(2)}) collective-permute-start(bf16[32,2,8,512]{3,2,1,0:T(8,128)(2,1)S(1)} %bitcast.225), channel_id=1, source_target_pairs={{0,1},{1,0},{2,3},{3,2},{4,5},{5,4},{6,7},{7,6},{8,9},{9,8},{10,11... | collective-permute-start | bytes 1572872 | tf_op jit(solution)/shard_map/ppermute | solution.py:96
  164.0 3.8 %copy-start.5 = (bf16[2,1,512,352]{2,1,0,3:T(2,128)(2,1)S(1)}, bf16[2,1,512,352]{2,1,0,3:T(2,128)(2,1)}, u32[]{:S(2)}) copy-start(bf16[2,1,512,352]{2,1,0,3:T(2,128)(2,1)} %get-tuple-element.10) | copy-start | bytes 2162692
  165.8 3.2 %copy-start.4 = (bf16[2,1,512,352]{2,1,0,3:T(2,128)(2,1)S(1)}, bf16[2,1,512,352]{2,1,0,3:T(2,128)(2,1)}, u32[]{:S(2)}) copy-start(bf16[2,1,512,352]{2,1,0,3:T(2,128)(2,1)} %get-tuple-element.22) | copy-start | bytes 2162692
  167.8 2.9 %copy-start.3 = (bf16[2,1,512,352]{2,1,0,3:T(2,128)(2,1)S(1)}, bf16[2,1,512,352]{2,1,0,3:T(2,128)(2,1)}, u32[]{:S(2)}) copy-start(bf16[2,1,512,352]{2,1,0,3:T(2,128)(2,1)} %get-tuple-element.9) | copy-start | bytes 2162692
  169.0 1.7 copy-start.7
  175.8 2.0 collective-permute-start.3
  177.8 30.3 %copy-start.1 = (bf16[1,2048,128]{2,1,0:T(8,128)(2,1)S(1)}, bf16[1,2048,128]{2,1,0:T(8,128)(2,1)}, u32[]{:S(2)}) copy-start(bf16[1,2048,128]{2,1,0:T(8,128)(2,1)} %param.18) | copy-start | bytes 1572868
  180.1 20.2 %all-to-all-start.5 = ((bf16[64,8,512]{2,1,0:T(8,128)(2,1)}), bf16[64,8,512]{2,1,0:T(8,128)(2,1)S(1)}, u32[]{:S(2)}, u32[]{:S(2)}) async-start(bf16[64,8,512]{2,1,0:T(8,128)(2,1)} %bitcast.74), calls=%async_computation.5 | async-start | bytes 1048576 | tf_op jit(solution)/shard_map/all_to_all | solution.py:86

commit v2 on v1

v2 whole, which is shorter than its diff:
```python
import functools
import math

import jax
import jax.numpy as jnp
from jax import lax
from jax.experimental import pallas as pl
from jax.experimental.pallas import tpu as pltpu
from jax.sharding import PartitionSpec as P

HD = 128
EXPERTS = 8
SPAN = 256
EPSILON = 1e-06
MASKED = -1e30
F32 = jnp.float32
BF16 = jnp.bfloat16
VM = pl.BlockSpec(memory_space=pltpu.VMEM)
SM = pl.BlockSpec(memory_space=pltpu.SMEM)
ANY = pl.BlockSpec(memory_space=pl.ANY)
ROWS_BY_ROWS = (((1,), (1,)), ((), ()))


def dot(a, b):
    return jnp.dot(a, b, preferred_element_type=F32)


def dot_rows(a, b):
    return lax.dot_general(a, b, ROWS_BY_ROWS, preferred_element_type=F32)


def call(body, out, ins, scratch=(), limit=40):
    many = isinstance(out, (list, tuple))
    return pl.pallas_call(
        body,
        out_shape=out,
        in_specs=ins,
        out_specs=[VM] * len(out) if many else VM,
        scratch_shapes=scratch,
        compiler_params=pltpu.CompilerParams(vmem_limit_bytes=limit << 20),
    )


def shape_of(shape, dtype=BF16):
    return jax.ShapeDtypeStruct(shape, dtype)


def message_kernel(slots, ids, tokens, gains, out):
    count, _, width = tokens.shape
    rows = 2 * count
    half = width // 2
    rank, core = lax.axis_index("req"), lax.axis_index("rep") % 2
    x = tokens[...].reshape(rows, width).astype(F32)
    scaling = lax.rsqrt(jnp.mean(x * x, axis=1, keepdims=True) + EPSILON)
    normed = (x * scaling * gains[0:1]).astype(BF16)
    out[0, :, :half] = jnp.where(core == 0, normed[:, :half], normed[:, half:])
    row = lax.broadcasted_iota(jnp.int32, (rows, HD), 0)
    lane = lax.broadcasted_iota(jnp.int32, (rows, HD), 1)
    notes = jnp.zeros((rows, HD), jnp.int32)
    for j in range(count):
        for s in range(2):
            here = row == 2 * j + s
            source = 2 * (rank * count + j) if s == 0 else 2 * slots[j] + 1
            notes = jnp.where(here & (lane == 0), source, notes)
            for k in range(2):
                notes = jnp.where(here & (lane == 1 + k), ids[0, s, k, j], notes)
    out[0, :, half:] = notes.astype(F32).astype(BF16)
    message = out[0]
    for r in range(1, out.shape[0]):
        out[r] = message


def order_of(near):
    peers, rows, wide = near.shape
    source = near[:, :, wide - HD :].reshape(peers * rows, HD)[:, :1]
    column = lax.broadcasted_iota(jnp.int32, (peers * rows, peers * rows), 1)
    return (source.astype(jnp.int32) == column).astype(BF16)


def query_kernel(near, far, wq, out):
    peers, rows, wide = near.shape
    half = wide - HD
    core = lax.axis_index("rep") % 2
    a = near[:, :, :half].reshape(peers * rows, half)
    b = far[:, :, :half].reshape(peers * rows, half)
    q = dot(a, wq[0, pl.ds(pl.multiple_of(core * half, half), half)])
    q = q + dot(b, wq[0, pl.ds(pl.multiple_of((1 - core) * half, half), half)])
    out[...] = dot(order_of(near), q.astype(BF16)).astype(BF16).reshape(out.shape)


def own_kernel(near, far, sel, own):
    peers, rows, wide = near.shape
    half = wide - HD
    rank, core = lax.axis_index("req"), lax.axis_index("rep") % 2
    source = near[rank][:, half : half + 1]
    column = lax.broadcasted_iota(jnp.int32, (rows, peers * rows), 1)
    order = (source.astype(jnp.int32) == column).astype(BF16)
    a = dot(order, near[...].reshape(peers * rows, wide))
    b = dot(order, far[:, :, :half].reshape(peers * rows, half)).astype(BF16)
    sel[...] = a[:, half:]
    a = a[:, :half].astype(BF16)
    own[:, :half] = jnp.where(core == 0, a, b)
    own[:, half:] = jnp.where(core == 0, b, a)


def page_kernel(table, lens, pool, out, sems):
    count, length = out.shape[:2]
    page = pool.shape[1]
    chunks = length // SPAN

    def each(act):
        for j in range(count):
            for c in range(chunks):
                pl.when(c * SPAN < lens[j])(functools.partial(act, j, c))

    def start(j, c):
        for p in range(SPAN // page):
            pltpu.make_async_copy(
                pool.at[table[j, c * (SPAN // page) + p]],
                out.at[j, pl.ds(c * SPAN + p * page, page)],
                sems.at[j, c],
            ).start()

    def wait(j, c):
        block = out.at[j, pl.ds(c * SPAN, SPAN)]
        pltpu.make_async_copy(block, block, sems.at[j, c]).wait()

    each(start)
    each(wait)


def attention_kernel(lens, sel, arrived, fresh, cache, out, qs, os, sc, ef):
    peers, rows, _ = arrived.shape
    count, _, _, wide = cache.shape
    heads = wide // HD
    group = 2 * heads
    inv_scale = 1.0 / math.sqrt(HD)
    picks = sel[...]
    masks = [[picks[:, 1 + k : 2 + k] == float(e) for e in range(EXPERTS)] for k in range(2)]
    for h in range(heads):
        values = [arrived[e * heads + h].astype(F32) for e in range(EXPERTS)]
        for k in range(2):
            total = jnp.where(masks[k][0], values[0], 0.0)
            for e in range(1, EXPERTS):
                total = total + jnp.where(masks[k][e], values[e], 0.0)
            qs[k * heads + h] = total
    ef[...] = jnp.zeros_like(ef)
    ef[0 : 2 * rows] = fresh[...].reshape(2 * rows, wide)
    extra = ef[...]
    big = (2 * group, wide)
    block_row = lax.broadcasted_iota(jnp.int32, big, 0) % heads
    diagonal = block_row == lax.broadcasted_iota(jnp.int32, big, 1) // HD
    scores_shape = (2 * group, 2 * SPAN)
    column = lax.broadcasted_iota(jnp.int32, scores_shape, 1)
    keys = column % 2 == 0
    e_col = lax.broadcasted_iota(jnp.int32, (2 * group, HD), 1)
    e_row = lax.broadcasted_iota(jnp.int32, (2 * group, HD), 0)
    requests = range(count)

    def block(j, c):
        return cache[j, pl.ds(c * SPAN, SPAN)].reshape(2 * SPAN, wide)

    def masked_scores(q, j, c):
        s = dot_rows(q, block(j, c)) * inv_scale
        return jnp.where(keys & (column < 2 * (lens[j] - c * SPAN)), s, MASKED)

    def highest(s):
        return jnp.max(s, axis=1, keepdims=True)

    def added(p):
        return jnp.sum(p, axis=1, keepdims=True)

    def onto_values(p):
        return pltpu.roll(p, 1, 1).astype(BF16)

    chunks = [(lens[j] + SPAN - 1) // SPAN for j in requests]
    queries, extras, firsts, tops = [], [], [], []
    for j in requests:
        q = jnp.concatenate([qs[:, 2 * j, :], qs[:, 2 * j + 1, :]], axis=0)
        q = jnp.where(diagonal, jnp.concatenate([q] * heads, axis=1), 0.0).astype(BF16)
        live = (e_col == 4 * j) | ((e_col == 4 * j + 2) & (e_row >= group))
        e = jnp.where(live, dot_rows(q, extra) * inv_scale, MASKED)
        s = masked_scores(q, j, 0)
        queries.append(q)
        extras.append(e)
        firsts.append(s)
        tops.append(jnp.maximum(highest(e), highest(s)))

    for j in requests:

        def score(c, top, j=j):
            s = masked_scores(queries[j], j, c)
            sc[j, c] = s
            return jnp.maximum(top, highest(s))

        tops[j] = lax.fori_loop(1, chunks[j], score, tops[j])

    extras = [jnp.exp(extras[j] - tops[j]) for j in requests]
    firsts = [jnp.exp(firsts[j] - tops[j]) for j in requests]
    sums = [added(extras[j]) + added(firsts[j]) for j in requests]
    for j in requests:

        def weigh(c, total, j=j):
            p = jnp.exp(sc[j, c] - tops[j])
            sc[j, c] = p
            return total + added(p)

        sums[j] = lax.fori_loop(1, chunks[j], weigh, sums[j])

    inverses = [1.0 / sums[j] for j in requests]
    mixed = [
        dot(onto_values(extras[j] * inverses[j]), extra)
        + dot(onto_values(firsts[j] * inverses[j]), block(j, 0))
        for j in requests
    ]
    for j in requests:

        def gather(c, total, j=j):
            return total + dot(onto_values(sc[j, c] * inverses[j]), block(j, c))

        mixed[j] = lax.fori_loop(1, chunks[j], gather, mixed[j])

    for j in requests:
        kept = jnp.where(diagonal, mixed[j], 0.0)
        o = kept[:, :HD]
        for h in range(1, heads):
            o = o + kept[:, h * HD : (h + 1) * HD]
        os[:, 2 * j, :] = o[:group]
        os[:, 2 * j + 1, :] = o[group:]
    for h in range(heads):
        first, second = os[h], os[heads + h]
        for e in range(EXPERTS):
            value = jnp.where(masks[0][e], first, 0.0) + jnp.where(masks[1][e], second, 0.0)
            out[e * heads + h] = value.astype(BF16)


def columns_of(z, core, quarter):
    return pl.ds(pl.multiple_of((2 * z + core) * quarter, quarter), quarter)


def project_kernel(near, returned, wo, answers, theirs):
    peers, halves, rows, quarter = theirs.shape
    core = lax.axis_index("rep") % 2
    values = returned[...].reshape(peers * rows, returned.shape[2])
    a = lax.dot_general(
        order_of(near), values, (((0,), (0,)), ((), ())), preferred_element_type=F32
    ).astype(BF16)
    answers[...] = a
    for z in range(halves):
        part = dot(a, wo[0, :, columns_of(z, 1 - core, quarter)])
        theirs[:, z] = part.astype(BF16).reshape(peers, rows, quarter)


def add_kernel(left, theirs, weight, out):
    peers, halves, rows, quarter = theirs.shape
    core = lax.axis_index("rep") % 2
    a = left[...]
    for z in range(halves):
        part = dot(a, weight[0, :, columns_of(z, core, quarter)]).reshape(peers, rows, quarter)
        out[:, z] = (part + theirs[:, z].astype(F32)).astype(BF16)


def expert_kernel(near, far, gains, wg, wu, wd, units, theirs):
    peers, halves, rows, quarter = near.shape
    core = lax.axis_index("rep") % 2
    total = peers * rows
    squares = jnp.zeros((total, 1), F32)
    for block in (near, far):
        for z in range(halves):
            v = block[:, z].reshape(total, quarter).astype(F32)
            squares = squares + jnp.sum(v * v, axis=1, keepdims=True)
    scaling = lax.rsqrt(squares / (2 * halves * quarter) + EPSILON)
    gate = jnp.zeros((total, wg.shape[1]), F32)
    up = jnp.zeros((total, wg.shape[1]), F32)
    for block, side in ((near, core), (far, 1 - core)):
        for z in range(halves):
            where = columns_of(z, side, quarter)
            v = block[:, z].reshape(total, quarter).astype(F32)
            v = (v * scaling * gains[1:2, where]).astype(BF16)
            gate = gate + dot_rows(v, wg[0, :, where])
            up = up + dot_rows(v, wu[0, :, where])
    a = (gate / (1.0 + jnp.exp(-gate)) * up).astype(BF16)
    units[...] = a
    for z in range(halves):
        part = dot(a, wd[0, :, columns_of(z, 1 - core, quarter)])
        theirs[:, z] = part.astype(BF16).reshape(peers, rows, quarter)


def shards(
    tokens,
    norm_gains,
    w_kv,
    w_query,
    w_out,
    w_gate,
    w_up,
    w_down,
    kv_pages,
    page_table,
    cache_len,
    route_ids,
    route_gates,
    new_slot,
):
    req_count = lax.axis_size("req")
    rep_count = lax.axis_size("rep")
    mine, _, width = tokens.shape
    rows = 2 * mine
    total = rows * req_count
    half = width // 2
    quarter = width // rep_count
    wide = kv_pages.shape[-1]
    rep = lax.axis_index("rep")
    swap = [(p, p ^ 1) for p in range(rep_count)]
    wide_groups = [
        [r * rep_count + 2 * z + c for r in range(req_count) for z in range(rep_count // 2)]
        for c in range(2)
    ]
    peers = req_count * rep_count // 2
    split = (req_count, rep_count // 2, rows, quarter)

    def spread_req(value):
        return lax.all_to_all(value, "req", split_axis=0, concat_axis=0, tiled=True)

    def spread_wide(value):
        return lax.all_to_all(
            value,
            ("req", "rep"),
            split_axis=0,
            concat_axis=0,
            tiled=True,
            axis_index_groups=wide_groups,
        )

    def other_core(value):
        return lax.ppermute(value, "rep", swap)

    inputs = tokens.reshape(rows, width)
    ids = route_ids.transpose(0, 2, 1, 3).reshape(rows, 2, 2)
    gates = route_gates.astype(F32).transpose(0, 2, 1, 3).reshape(rows, 2, 2)
    experts_row = jnp.arange(EXPERTS, dtype=jnp.int32)
    shares = jnp.sum(jnp.where(ids[..., None] == experts_row, gates[..., None], 0.0), axis=2)

    message = call(message_kernel, shape_of((req_count, rows, half + HD)), [SM, SM, VM, VM])(
        new_slot, route_ids.transpose(1, 2, 3, 0), tokens, norm_gains
    )
    near = spread_req(message)
    length = page_table.shape[1] * kv_pages.shape[1]
    cache = call(
        page_kernel,
        pltpu.VMEM((mine, length) + kv_pages.shape[2:], BF16),
        [SM, SM, ANY],
        [pltpu.SemaphoreType.DMA((mine, length // SPAN))],
        20,
    )(page_table, cache_len, kv_pages)
    far = other_core(near)
    ordered = call(query_kernel, shape_of((req_count, rows, HD)), [VM] * 3)(near, far, w_query)
    arrived = spread_req(ordered)
    sel, own = call(own_kernel, [shape_of((rows, HD), F32), shape_of((rows, width))], [VM] * 2)(
        near, far
    )
    fresh = jnp.einsum("rd,dtc->rtc", own, w_kv, preferred_element_type=F32).astype(BF16)
    back = call(
        attention_kernel,
        shape_of((req_count, rows, HD)),
        [SM, VM, VM, VM, VM],
        [
            pltpu.VMEM((2 * wide // HD, rows, HD), F32),
            pltpu.VMEM((2 * wide // HD, rows, HD), F32),
            pltpu.VMEM((mine, length // SPAN, 4 * wide // HD, 2 * SPAN), F32),
            pltpu.VMEM((HD, wide), BF16),
        ],
        20,
    )(cache_len, sel, arrived, fresh, cache)
    returned = spread_req(back)
    answers, theirs = call(
        project_kernel, [shape_of((total, w_out.shape[1])), shape_of(split)], [VM] * 3
    )(near, returned, w_out)

    def reduce_wide(left, theirs, weight, share):
        summed = call(add_kernel, shape_of(split), [VM] * 3)(left, other_core(theirs), weight)
        got = spread_wide(summed.reshape(peers, rows, quarter))
        got = got.reshape(EXPERTS, peers // EXPERTS, rows, quarter).astype(F32)
        return jnp.sum(jnp.sum(got, axis=1) * share.T[:, :, None], axis=0)

    kept = lax.dynamic_slice_in_dim(inputs, rep * quarter, quarter, 1).astype(F32)
    hidden = kept + reduce_wide(answers, theirs, w_out, shares[:, 0])
    block = spread_wide(jnp.broadcast_to(hidden.astype(BF16)[None], (peers, rows, quarter)))
    units, theirs = call(
        expert_kernel, [shape_of((total, w_down.shape[1])), shape_of(split)], [VM] * 6
    )(
        block.reshape(split),
        other_core(block).reshape(split),
        norm_gains,
        w_gate.transpose(0, 2, 1),
        w_up.transpose(0, 2, 1),
        w_down,
    )
    feed = reduce_wide(units, theirs, w_down, shares[:, 1])
    final = lax.all_gather((hidden + feed).astype(BF16), "rep", axis=1, tiled=True)
    return final.reshape(mine, 2, width)


def solution(mesh):
    in_specs = (
        P("req", None, None),
        P(),
        P(None, None, "rep"),
        P("req", None, "rep"),
        P("req", "rep", None),
        P("req", None, "rep"),
        P("req", None, "rep"),
        P("req", "rep", None),
        P("req", None, None, "rep"),
        P("req", None),
        P("req"),
        P("req", None, None, None),
        P("req", None, None, None),
        P("req"),
    )
    out_specs = P("req", None, None)
    return jax.shard_map(shards, mesh=mesh, in_specs=in_specs, out_specs=out_specs, check_vma=False)
```

time: 210 us -> 155 us (0.74)
  local copies, waits for them, and re-layouts: 80.6 us -> 18.2 us
  blocking collectives: 6.99 us -> 60.8 us
  starting transfers between devices: 50.1 us -> 23.7 us
  matrix products: 20.5 us -> 2.86 us
  Pallas kernels: 0 us -> 14.4 us
  waiting for transfers between devices: 41.7 us -> 33.3 us
  other arithmetic: 7.68 us -> 0.41 us
    all_to_all x0 -> x3, blocking collectives: none -> 53.7 us  [the longest x2 38.2 us: spread_req(): return lax.all_to_all(value, 'req', split_axis=0, concat_axis=0, tiled=True)]
    gather x1 -> x0, local copies, waits for them, and re-layouts: 25.4 us -> none  [shards(): pages = kv_pages[page_table].reshape(mine, -1, 2, heads_rep, HD)]
    reshape x8 -> x2, local copies, waits for them, and re-layouts: 23.5 us -> 0.66 us  [the longest x1 0.65 us: shards(): return final.reshape(mine, 2, width)]
    all_to_all x3 -> x1, starting transfers between devices: 25.5 us -> 5.75 us  [spread_req(): return lax.all_to_all(value, 'req', split_axis=0, concat_axis=0, tiled=True)]
    dot_general x15 -> x1, matrix products: 20.5 us -> 2.86 us  [shards(): jnp.einsum('rd,dtc->rtc', own, w_kv, preferred_element_type=F32)]
    unnamed x30 -> x38, local copies, waits for them, and re-layouts: 0.13 us -> 16.9 us
    pallas_call x0 -> x9, Pallas kernels: none -> 14.4 us  [the longest x1 4.56 us: shards(): call(page_kernel, pltpu.VMEM((mine, length) + kv_pages.shape[2:], BF16),...]
    slice x3 -> x0, local copies, waits for them, and re-layouts: 8.98 us -> none  [the longest x1 8.1 us: shards(): pages[:, :, 0]]
  transfers between devices with their start and end apart: 10 -> 7, of which waited for: 8 -> 6; matrix products, arithmetic and copies ran while one was open for 38% -> 2% of each run, Pallas kernels for 0% -> 3%
where the time goes in v2:
time: 155 us; the launch traced here: 154 us
  blocking collectives  60.8 us (39%)
  waiting for transfers between devices  33.3 us (21%)
  starting transfers between devices  23.7 us (15%)
  local copies, waits for them, and re-layouts  18.2 us (12%)
  Pallas kernels  14.4 us (9%)
  matrix products  2.86 us (2%)
    all_to_all x2, blocking collectives, spread_req(): return lax.all_to_all(value, 'req', split_axis=0, concat_axis=0, tiled=True)  38.2 us
    all_to_all x2, waiting for transfers between devices, spread_wide(): lax.all_to_all(value, ('req', 'rep'), split_axis=0, concat_axis=0, tiled=...  23.3 us
    unnamed x38, local copies, waits for them, and re-layouts  16.9 us
    all_to_all x1, blocking collectives, spread_wide(): lax.all_to_all(value, ('req', 'rep'), split_axis=0, concat_axis=0, tiled=...  15.5 us
    all_to_all x2, starting transfers between devices, spread_wide(): lax.all_to_all(value, ('req', 'rep'), split_axis=0, concat_axis=0, tiled=...  9.27 us
    ppermute x4, starting transfers between devices, other_core(): return lax.ppermute(value, 'rep', swap)  8.66 us
    all_gather x1, blocking collectives, shards(): lax.all_gather((hidden + feed).astype(BF16), 'rep', axis=1, tiled=True)  7.08 us
    all_to_all x1, starting transfers between devices, spread_req(): return lax.all_to_all(value, 'req', split_axis=0, concat_axis=0, tiled=True)  5.75 us
  transfers between devices with their start and end apart: 7, of which 6 were waited for; matrix products, arithmetic and copies ran while one was open for 2% of the time, Pallas kernels for 3%

profile of v2, /device:TPU:1, one launch (start us, length us, event | category | flops | bytes accessed | tf_op | source)
XLA Modules:
  0.0 153.8 jit_solution(1383738524298708499)
XLA Ops:
  0.0 0.0 copy-start.8
  0.0 0.8 copy-done.8
  0.8 0.0 copy-start.10
  0.8 0.7 copy-done.10
  1.5 0.7 copy-done.12
  2.2 0.7 copy-done.17
  2.8 0.8 shard_map.136
  3.6 24.0 %all_to_all.30.near = bf16[32,8,1152]{2,1,0:T(8,128)(2,1)S(1)} all-to-all(bf16[32,8,1152]{2,1,0:T(8,128)(2,1)S(1)} %shard_map.136), channel_id=1, replica_groups=mesh['req'=32,'rep'=4] {'req'}, dimensions={0} | all-to-all | bytes 1179648 | tf_op jit(solution)/shard_map/all_to_all | solution.py:323
  27.6 2.2 %collective-permute-start = (bf16[32,8,1152]{2,1,0:T(8,128)(2,1)S(1)}, bf16[32,8,1152]{2,1,0:T(8,128)(2,1)S(1)}, u32[]{:S(2)}, u32[]{:S(2)}) collective-permute-start(bf16[32,8,1152]{2,1,0:T(8,128)(2,1)S(1)} %all_to_all.30.near), channel_id=1, source_target_pairs={{0,1},{1,0},{2,3},{3,2},{4,5},{5,4},{6,7},{7,6},{8,9},{9,8},{10,11... | collective-permute-start | bytes 1769480 | tf_op jit(solution)/shard_map/ppermute | solution.py:336
  29.7 3.4 %copy-done.2 = bf16[256,16,2,512]{3,2,1,0:T(2,128)(2,1)S(1)} copy-done((bf16[256,16,2,512]{3,2,1,0:T(2,128)(2,1)S(1)}, bf16[256,16,2,512]{3,2,1,0:T(2,128)(2,1)}, u32[]{:S(2)}) %copy-start.2) | copy-done | bytes 8388632
  33.1 0.7 copy-done.14
  33.8 0.7 copy-done.16
  34.5 4.6 %shard_map.139.cache = bf16[4,1024,2,512]{3,2,1,0:T(2,128)(2,1)S(1)} custom-call(s32[4,64]{1,0:T(4,128)S(1)} %copy-done.16, s32[4]{0:T(128)S(1)} %copy-done.14, bf16[256,16,2,512]{3,2,1,0:T(2,128)(2,1)S(1)} %copy-done.2), custom_call_target="tpu_custom_call" | custom-call | tf_op jit(solution)/shard_map/pallas_call | solution.py:349
  39.0 0.0 copy-start
  39.0 3.2 %copy-done = bf16[4,1024,2,512]{3,2,1,0:T(2,128)(2,1)} copy-done((bf16[4,1024,2,512]{3,2,1,0:T(2,128)(2,1)}, bf16[4,1024,2,512]{3,2,1,0:T(2,128)(2,1)S(1)}, u32[]{:S(2)}) %copy-start) | copy-done | bytes 8388632
  42.3 0.0 collective-permute-done.far
  42.3 0.0 copy-done.7
  42.3 1.3 shard_map.138
  43.5 5.7 %all-to-all-start.1 = ((bf16[32,8,128]{2,1,0:T(8,128)(2,1)}), bf16[32,8,128]{2,1,0:T(8,128)(2,1)S(1)}, u32[]{:S(2)}, u32[]{:S(2)}) async-start(bf16[32,8,128]{2,1,0:T(8,128)(2,1)} %shard_map.138), calls=%async_computation.1 | async-start | bytes 131072 | tf_op jit(solution)/shard_map/all_to_all | solution.py:323
  49.3 0.3 shard_map.137
  49.6 2.9 %fusion = bf16[8,2,512]{2,0,1:T(8,128)(2,1)S(1)} fusion(bf16[2048,2,512]{2,1,0:T(2,128)(2,1)} %param.16, bf16[8,2048]{1,0:T(8,128)(2,1)S(1)} %get-tuple-element.12), kind=kOutput, calls=%fused_computation | convolution fusion | flops 33554432 | bytes 4243456 | tf_op jit(solution)/shard_map/rd,dtc->rtc/dot_general | solution.py:362
  52.5 5.4 %all-to-all-done.1.arrived = bf16[32,8,128]{2,1,0:T(8,128)(2,1)S(1)} async-done(((bf16[32,8,128]{2,1,0:T(8,128)(2,1)}), bf16[32,8,128]{2,1,0:T(8,128)(2,1)S(1)}, u32[]{:S(2)}, u32[]{:S(2)}) %all-to-all-start.1) | async-done | bytes 65568 | tf_op jit(solution)/shard_map/all_to_all | solution.py:323
  57.9 0.0 copy-done.15
  57.9 3.4 %copy-done.1 = bf16[4,1024,2,512]{3,2,1,0:T(2,128)(2,1)S(1)} copy-done((bf16[4,1024,2,512]{3,2,1,0:T(2,128)(2,1)S(1)}, bf16[4,1024,2,512]{3,2,1,0:T(2,128)(2,1)}, u32[]{:S(2)}) %copy-start.1) | copy-done | bytes 8388632
  61.3 2.8 %shard_map.140 = bf16[32,8,128]{2,1,0:T(8,128)(2,1)S(1)} custom-call(s32[4]{0:T(128)S(1)} %copy-done.15, f32[8,128]{1,0:T(8,128)S(1)} %get-tuple-element.11.sel, bf16[32,8,128]{2,1,0:T(8,128)(2,1)S(1)} %all-to-all-done.1.arrived, bf16[8,2,512]{2,1,0:T(2,128)(2,1)S(1)} %copy.40.fresh, bf16[4,1024,2,512]{3,2,1,0:T(2,128)(2,1)S(1)} %copy-done.1), custom_call_target="tpu_custom_call" | custom-call | tf_op jit(solution)/shard_map/pallas_call | solution.py:363
  64.2 0.0 copy-start.3
  64.2 0.0 copy-start.11
  64.2 14.2 %all_to_all.31.returned = bf16[32,8,128]{2,1,0:T(8,128)(2,1)S(1)} all-to-all(bf16[32,8,128]{2,1,0:T(8,128)(2,1)S(1)} %shard_map.140), channel_id=1, replica_groups=mesh['req'=32,'rep'=4] {'req'}, dimensions={0} | all-to-all | bytes 131072 | tf_op jit(solution)/shard_map/all_to_all | solution.py:323
  78.4 0.0 copy-done.4
  78.4 0.5 shard_map.141
  79.0 2.8 %collective-permute-start.1 = (bf16[32,2,8,512]{3,2,1,0:T(8,128)(2,1)S(1)}, bf16[32,2,8,512]{3,2,1,0:T(8,128)(2,1)S(1)}, u32[]{:S(2)}, u32[]{:S(2)}) collective-permute-start(bf16[32,2,8,512]{3,2,1,0:T(8,128)(2,1)S(1)} %get-tuple-element.14), channel_id=1, source_target_pairs={{0,1},{1,0},{2,3},{3,2},{4,5},{5,4},{6,7},{7,6},{8,9},{9,8},{10,11... | collective-permute-start | bytes 1572872 | tf_op jit(solution)/shard_map/ppermute | solution.py:336
  81.7 0.0 copy-done.9
  81.8 1.5 collective-permute-done.1.theirs
  83.3 1.1 shard_map.142
  84.4 4.6 %all-to-all-start.3 = ((bf16[64,8,512]{2,1,0:T(8,128)(2,1)}), bf16[64,8,512]{2,1,0:T(8,128)(2,1)S(1)}, u32[]{:S(2)}, u32[]{:S(2)}) async-start(bf16[64,8,512]{2,1,0:T(8,128)(2,1)} %bitcast.2), calls=%async_computation.3 | async-start | bytes 1048576 | tf_op jit(solution)/shard_map/all_to_all | solution.py:326
  89.0 0.0 copy-done.18
  89.0 0.1 copy.34
  89.1 0.1 reshape.36
  89.2 0.0 copy-done.13
  89.2 0.1 copy.33
  89.3 0.1 eq.15
  89.4 0.1 select_reduce_fusion
  89.5 0.1 copy.35
  89.6 11.4 %all-to-all-done.3 = bf16[64,8,512]{2,1,0:T(8,128)(2,1)S(1)} async-done(((bf16[64,8,512]{2,1,0:T(8,128)(2,1)}), bf16[64,8,512]{2,1,0:T(8,128)(2,1)S(1)}, u32[]{:S(2)}, u32[]{:S(2)}) %all-to-all-start.3) | async-done | bytes 524320 | tf_op jit(solution)/shard_map/all_to_all | solution.py:326
  101.0 0.1 convert_reduce_fusion.1
  101.1 0.1 multiply_reduce_fusion.1
  101.2 15.5 %all_to_all.32 = bf16[64,8,512]{2,1,0:T(8,128)(2,1)S(1)} all-to-all(bf16[64,8,512]{2,1,0:T(8,128)(2,1)S(1)} %broadcast_in_dim.30), channel_id=1, replica_groups={{0,2,4,6,8,10,12,14,16,18,20,22,24,26,28,30,32,34,36,38,40,42,44,46,48,..., dimensions={0} | all-to-all | bytes 1048576 | tf_op jit(solution)/shard_map/all_to_all | solution.py:326
  116.7 3.2 %collective-permute-start.2 = (bf16[64,8,512]{2,1,0:T(8,128)(2,1)S(1)}, bf16[64,8,512]{2,1,0:T(8,128)(2,1)S(1)}, u32[]{:S(2)}, u32[]{:S(2)}) collective-permute-start(bf16[64,8,512]{2,1,0:T(8,128)(2,1)S(1)} %all_to_all.32), channel_id=1, source_target_pairs={{0,1},{1,0},{2,3},{3,2},{4,5},{5,4},{6,7},{7,6},{8,9},{9,8},{10,11... | collective-permute-start | bytes 1572872 | tf_op jit(solution)/shard_map/ppermute | solution.py:336
  119.9 1.5 collective-permute-done.2
  121.5 0.0 copy-done.3
  121.5 0.0 copy-done.11
  121.5 1.4 copy-done.5
  122.8 1.4 copy-done.6
  124.2 1.8 %shard_map.143 = (bf16[256,352]{1,0:T(8,128)(2,1)S(1)}, bf16[32,2,8,512]{3,2,1,0:T(8,128)(2,1)S(1)}) custom-call(bf16[32,2,8,512]{3,2,1,0:T(8,128)(2,1)S(1)} %bitcast.31, bf16[32,2,8,512]{3,2,1,0:T(8,128)(2,1)S(1)} %bitcast.34, f32[2,2048]{1,0:T(2,128)S(1)} %copy-done.11, bf16[1,352,2048]{2,1,0:T(8,128)(2,1)S(1)} %bitcast.32, ...), custom_call_target="tpu_custom_call" | custom-call | tf_op jit(solution)/shard_map/pallas_call | solution.py:389
  126.0 0.5 collective-permute-start.3
  126.5 1.5 collective-permute-done.3.theirs
  128.0 1.3 shard_map.144
  129.3 4.6 %all-to-all-start.5 = ((bf16[64,8,512]{2,1,0:T(8,128)(2,1)}), bf16[64,8,512]{2,1,0:T(8,128)(2,1)S(1)}, u32[]{:S(2)}, u32[]{:S(2)}) async-start(bf16[64,8,512]{2,1,0:T(8,128)(2,1)} %bitcast.12), calls=%async_computation.5 | async-start | bytes 1048576 | tf_op jit(solution)/shard_map/all_to_all | solution.py:326
  133.9 0.1 copy.36
  134.0 11.9 %all-to-all-done.5 = bf16[64,8,512]{2,1,0:T(8,128)(2,1)S(1)} async-done(((bf16[64,8,512]{2,1,0:T(8,128)(2,1)}), bf16[64,8,512]{2,1,0:T(8,128)(2,1)S(1)}, u32[]{:S(2)}, u32[]{:S(2)}) %all-to-all-start.5) | async-done | bytes 524320 | tf_op jit(solution)/shard_map/all_to_all | solution.py:326
  145.9 0.1 convert_reduce_fusion
  146.0 0.1 multiply_reduce_fusion
  146.1 7.1 %all_gather.3 = bf16[8,2048]{1,0:T(8,128)(2,1)S(1)} all-gather(bf16[8,512]{1,0:T(8,128)(2,1)S(1)} %add_convert_fusion), channel_id=1, replica_groups=mesh['req'=32,'rep'=4] {'rep'}, dimensions={1}, use_global_device_ids=true | all-gather | bytes 40960 | tf_op jit(solution)/shard_map/all_gather | solution.py:400
  153.2 0.6 reshape.34
  (21 shorter events, 0.1 us)
Async XLA Ops:
  0.0 0.8 copy-start.8
  0.8 0.7 copy-start.10
  1.5 0.7 copy-start.12
  2.2 0.7 copy-start.17
  27.6 14.7 %collective-permute-start = (bf16[32,8,1152]{2,1,0:T(8,128)(2,1)S(1)}, bf16[32,8,1152]{2,1,0:T(8,128)(2,1)S(1)}, u32[]{:S(2)}, u32[]{:S(2)}) collective-permute-start(bf16[32,8,1152]{2,1,0:T(8,128)(2,1)S(1)} %all_to_all.30.near), channel_id=1, source_target_pairs={{0,1},{1,0},{2,3},{3,2},{4,5},{5,4},{6,7},{7,6},{8,9},{9,8},{10,11... | collective-permute-start | bytes 1769480 | tf_op jit(solution)/shard_map/ppermute | solution.py:336
  29.7 3.4 %copy-start.2 = (bf16[256,16,2,512]{3,2,1,0:T(2,128)(2,1)S(1)}, bf16[256,16,2,512]{3,2,1,0:T(2,128)(2,1)}, u32[]{:S(2)}) copy-start(bf16[256,16,2,512]{3,2,1,0:T(2,128)(2,1)} %pool.1) | copy-start | bytes 25165828
  33.1 0.7 copy-start.14
  33.8 0.7 copy-start.16
  34.5 7.8 %copy-start.7 = (bf16[1,2048,128]{2,1,0:T(8,128)(2,1)S(1)}, bf16[1,2048,128]{2,1,0:T(8,128)(2,1)}, u32[]{:S(2)}) copy-start(bf16[1,2048,128]{2,1,0:T(8,128)(2,1)} %wq.1) | copy-start | bytes 1572868
  39.0 3.2 %copy-start = (bf16[4,1024,2,512]{3,2,1,0:T(2,128)(2,1)}, bf16[4,1024,2,512]{3,2,1,0:T(2,128)(2,1)S(1)}, u32[]{:S(2)}) copy-start(bf16[4,1024,2,512]{3,2,1,0:T(2,128)(2,1)S(1)} %shard_map.139.cache) | copy-start | bytes 25165828
  42.3 15.7 %copy-start.15 = (s32[4]{0:T(128)S(1)}, s32[4]{0:T(128)}, u32[]{:S(2)}) copy-start(s32[4]{0:T(128)} %lens.3) | copy-start | bytes 52
  43.5 14.4 %all-to-all-start.1 = ((bf16[32,8,128]{2,1,0:T(8,128)(2,1)}), bf16[32,8,128]{2,1,0:T(8,128)(2,1)S(1)}, u32[]{:S(2)}, u32[]{:S(2)}) async-start(bf16[32,8,128]{2,1,0:T(8,128)(2,1)} %shard_map.138), calls=%async_computation.1 | async-start | bytes 131072 | tf_op jit(solution)/shard_map/all_to_all | solution.py:323
  57.9 3.4 %copy-start.1 = (bf16[4,1024,2,512]{3,2,1,0:T(2,128)(2,1)S(1)}, bf16[4,1024,2,512]{3,2,1,0:T(2,128)(2,1)}, u32[]{:S(2)}) copy-start(bf16[4,1024,2,512]{3,2,1,0:T(2,128)(2,1)} %copy-done) | copy-start | bytes 25165828
  61.3 17.1 %copy-start.4 = (bf16[1,128,2048]{2,1,0:T(8,128)(2,1)S(1)}, bf16[1,128,2048]{2,1,0:T(8,128)(2,1)}, u32[]{:S(2)}) copy-start(bf16[1,128,2048]{2,1,0:T(8,128)(2,1)} %weight.2) | copy-start | bytes 1572868
  61.3 20.4 %copy-start.9 = (bf16[4,2,2048]{2,1,0:T(2,128)(2,1)S(1)}, bf16[4,2,2048]{2,1,0:T(2,128)(2,1)}, u32[]{:S(2)}) copy-start(bf16[4,2,2048]{2,1,0:T(2,128)(2,1)} %tokens.1) | copy-start | bytes 98308
  61.3 27.7 %copy-start.18 = (bf16[4,2,2,2]{0,3,2,1:T(2,128)(2,1)S(1)}, bf16[4,2,2,2]{0,3,2,1:T(2,128)(2,1)}, u32[]{:S(2)}) copy-start(bf16[4,2,2,2]{0,3,2,1:T(2,128)(2,1)} %param.26) | copy-start | bytes 196
  61.3 27.9 %copy-start.13 = (s32[4,2,2,2]{0,3,2,1:T(2,128)S(1)}, s32[4,2,2,2]{0,3,2,1:T(2,128)}, u32[]{:S(2)}) copy-start(s32[4,2,2,2]{0,3,2,1:T(2,128)} %param.25) | copy-start | bytes 388
  64.2 57.3 %copy-start.3 = (bf16[1,352,2048]{2,1,0:T(8,128)(2,1)S(1)}, bf16[1,352,2048]{2,1,0:T(8,128)(2,1)}, u32[]{:S(2)}) copy-start(bf16[1,352,2048]{2,1,0:T(8,128)(2,1)} %weight.3) | copy-start | bytes 4325380
  64.2 57.3 %copy-start.11 = (f32[2,2048]{1,0:T(2,128)S(1)}, f32[2,2048]{1,0:T(2,128)}, u32[]{:S(2)}) copy-start(f32[2,2048]{1,0:T(2,128)} %gains.3) | copy-start | bytes 49156
  79.0 4.3 %collective-permute-start.1 = (bf16[32,2,8,512]{3,2,1,0:T(8,128)(2,1)S(1)}, bf16[32,2,8,512]{3,2,1,0:T(8,128)(2,1)S(1)}, u32[]{:S(2)}, u32[]{:S(2)}) collective-permute-start(bf16[32,2,8,512]{3,2,1,0:T(8,128)(2,1)S(1)} %get-tuple-element.14), channel_id=1, source_target_pairs={{0,1},{1,0},{2,3},{3,2},{4,5},{5,4},{6,7},{7,6},{8,9},{9,8},{10,11... | collective-permute-start | bytes 1572872 | tf_op jit(solution)/shard_map/ppermute | solution.py:336
  84.4 16.6 %all-to-all-start.3 = ((bf16[64,8,512]{2,1,0:T(8,128)(2,1)}), bf16[64,8,512]{2,1,0:T(8,128)(2,1)S(1)}, u32[]{:S(2)}, u32[]{:S(2)}) async-start(bf16[64,8,512]{2,1,0:T(8,128)(2,1)} %bitcast.2), calls=%async_computation.3 | async-start | bytes 1048576 | tf_op jit(solution)/shard_map/all_to_all | solution.py:326
  116.7 4.8 %collective-permute-start.2 = (bf16[64,8,512]{2,1,0:T(8,128)(2,1)S(1)}, bf16[64,8,512]{2,1,0:T(8,128)(2,1)S(1)}, u32[]{:S(2)}, u32[]{:S(2)}) collective-permute-start(bf16[64,8,512]{2,1,0:T(8,128)(2,1)S(1)} %all_to_all.32), channel_id=1, source_target_pairs={{0,1},{1,0},{2,3},{3,2},{4,5},{5,4},{6,7},{7,6},{8,9},{9,8},{10,11... | collective-permute-start | bytes 1572872 | tf_op jit(solution)/shard_map/ppermute | solution.py:336
  121.5 1.4 copy-start.5
  122.8 1.4 copy-start.6
  126.0 2.0 %collective-permute-start.3 = (bf16[32,2,8,512]{3,2,1,0:T(8,128)(2,1)S(1)}, bf16[32,2,8,512]{3,2,1,0:T(8,128)(2,1)S(1)}, u32[]{:S(2)}, u32[]{:S(2)}) collective-permute-start(bf16[32,2,8,512]{3,2,1,0:T(8,128)(2,1)S(1)} %get-tuple-element.16), channel_id=1, source_target_pairs={{0,1},{1,0},{2,3},{3,2},{4,5},{5,4},{6,7},{7,6},{8,9},{9,8},{10,11... | collective-permute-start | bytes 1572872 | tf_op jit(solution)/shard_map/ppermute | solution.py:336
  129.3 16.6 %all-to-all-start.5 = ((bf16[64,8,512]{2,1,0:T(8,128)(2,1)}), bf16[64,8,512]{2,1,0:T(8,128)(2,1)S(1)}, u32[]{:S(2)}, u32[]{:S(2)}) async-start(bf16[64,8,512]{2,1,0:T(8,128)(2,1)} %bitcast.12), calls=%async_computation.5 | async-start | bytes 1048576 | tf_op jit(solution)/shard_map/all_to_all | solution.py:326
